TPU v7x, 512 devices: a whole 4x4x16 slice. The times are simulated.
512 devices in a mesh: crop: 4 (over y), space: 128 (over x, z, core).
Axes of the slice: x: 4, y: 4, z: 16, core: 2. Of those that a mesh axis runs over, the one named last changes fastest.
Arguments:
- features: bfloat16 [2048, 8, 8, 192], P(('crop', 'space')), parts along dimension 0, may hold values from -6 to 6
- cotangent: bfloat16 [2048, 8, 8, 192], P(('crop', 'space')), parts along dimension 0, may hold values from -6 to 6
- kernel: float32 [7, 7, 7, 192], replicated, may hold values from -0.3125 to 0.3125
- b_dw: float32 [192], replicated, may hold values from -3 to 3
- ln_gain: float32 [192], replicated, may hold values from 0.5 to 1.5
- ln_bias: float32 [192], replicated, may hold values from -3 to 3
- w_in_t: bfloat16 [768, 192], P('space'), may hold values from -0.4375 to 0.4375
- b_in: bfloat16 [768], P('space'), may hold values from -3 to 3
- w_out: bfloat16 [768, 192], P('space'), may hold values from -0.21875 to 0.21875
- b_out: float32 [192], replicated, may hold values from -3 to 3
- gamma: float32 [192], replicated, may hold values from 0.5 to 1.5
Outputs:
- block_out: bfloat16 [2048, 8, 8, 192], P(('crop', 'space')), parts along dimension 0
- d_x: bfloat16 [2048, 8, 8, 192], P(('crop', 'space')), parts along dimension 0
- d_kernel: float32 [28, 7, 7, 192], P('crop'), parts along dimension 0
- d_b_dw: float32 [768], P('crop'), parts along dimension 0
- d_ln_gain: float32 [768], P('crop'), parts along dimension 0
- d_ln_bias: float32 [768], P('crop'), parts along dimension 0
- d_w_in: float32 [3072, 192], P(('crop', 'space')), parts along dimension 0
- d_b_in: float32 [3072], P(('crop', 'space')), parts along dimension 0
- d_w_out: float32 [3072, 192], P(('crop', 'space')), parts along dimension 0
- d_b_out: float32 [768], P('crop'), parts along dimension 0
- d_gamma: float32 [768], P('crop'), parts along dimension 0
There are 4 independent parts, one for each index of `crop`. A program takes and returns all parts, laid end to end along the dimension named above; an argument that names none is the same for every part. Nothing has to cross between parts.
All inputs are finite; a program needn't handle non-finite values.
Results may differ from a plain program's by a relative error of at most 0.0065.
Values may be sent and summed in bfloat16 or wider, within the bound.
A program may use at most 64 MiB of HBM per device.

v0:
```python
import jax
import jax.numpy as jnp
from jax import lax
from jax.sharding import PartitionSpec as P

root_half = 0.7071067811865476
inv_root_tau = 0.3989422804014327


def padded_2(x, sides, width):
    for axis, dim in sides:
        size, length = (lax.axis_size(axis), x.shape[dim])
        up = [(i, (i + 1) % size) for i in range(size - 1)]
        down = [(j, i) for i, j in up]
        last = lax.slice_in_dim(x, length - width, length, axis=dim)
        initial = lax.slice_in_dim(x, 0, width, axis=dim)
        before = lax.ppermute(last, axis, up)
        after = lax.ppermute(initial, axis, down)
        x = jnp.concatenate([before, x, after], axis=dim)
    return x


def gelu_value(pre):
    return 0.5 * pre * (1.0 + lax.erf(pre * root_half))


def gelu_slope(pre):
    return 0.5 * (1.0 + lax.erf(pre * root_half)) + pre * jnp.exp(-0.5 * pre * pre) * inv_root_tau


def stencil(padded, kernel, size_x, size_y, size_z):
    width = kernel.shape[0]
    chans = padded.shape[3]

    def stencil_over_x(along_x, total):
        plane = lax.dynamic_slice_in_dim(padded, along_x, size_x, 0)
        taps_x = lax.dynamic_index_in_dim(kernel, along_x, 0, keepdims=False)

        def stencil_over_y(along_y, inner):
            strip = lax.dynamic_slice_in_dim(plane, along_y, size_y, 1)
            taps_y = lax.dynamic_index_in_dim(taps_x, along_y, 0, keepdims=False)
            for along_z in range(width):
                window = strip[:, :, along_z : along_z + size_z]
                inner = inner + window.astype(jnp.float32) * taps_y[along_z]
            return inner

        return lax.fori_loop(0, width, stencil_over_y, total)

    start = jnp.zeros((size_x, size_y, size_z, chans), jnp.float32)
    return lax.fori_loop(0, width, stencil_over_x, start)


def kernel_terms(padded, grad, width):
    size_x, size_y, size_z, chans = grad.shape
    grad_f = grad.astype(jnp.float32)

    def kernel_over_x(along_x):
        plane = lax.dynamic_slice_in_dim(padded, along_x, size_x, 0)

        def kernel_over_y(along_y):
            strip = lax.dynamic_slice_in_dim(plane, along_y, size_y, 1)
            terms = []
            for along_z in range(width):
                window = strip[:, :, along_z : along_z + size_z]
                terms.append(jnp.sum(window.astype(jnp.float32) * grad_f, axis=(0, 1, 2)))
            return jnp.stack(terms)

        return lax.map(kernel_over_y, jnp.arange(width, dtype=jnp.int32))

    return lax.map(kernel_over_x, jnp.arange(width, dtype=jnp.int32))


def side_pad(field, half):
    return jnp.pad(field, ((0, 0), (half, half), (half, half), (0, 0)))


def on_device(
    features, cotangent, kernel, b_dw, ln_gain, ln_bias, w_in_t, b_in, w_out, b_out, gamma
):
    size_x, size_y, size_z, chans = features.shape
    width = kernel.shape[0]
    half = width // 2
    scale = float(size_x * lax.axis_size("space") * size_y * size_z) ** (-0.5)
    rows = size_x * size_y * size_z
    with_rim = padded_2(features, (("space", 0),), half)
    padded = side_pad(with_rim, half)
    mixed = stencil(padded, kernel, size_x, size_y, size_z) + b_dw
    centred = mixed - jnp.mean(mixed, axis=-1, keepdims=True)
    inverse = lax.rsqrt(jnp.mean(centred * centred, axis=-1, keepdims=True) + 1e-06)
    unit_value = centred * inverse
    normed = (unit_value * ln_gain + ln_bias).astype(jnp.bfloat16)
    normed_rows = normed.reshape(rows, chans)
    w_in_all, b_in_all, w_out_all = (
        lax.all_gather(w_in_t, "space", axis=0, tiled=True),
        lax.all_gather(b_in, "space", axis=0, tiled=True),
        lax.all_gather(w_out, "space", axis=0, tiled=True),
    )
    pre = lax.dot_general(
        normed_rows, w_in_all, (((1,), (1,)), ((), ())), preferred_element_type=jnp.float32
    )
    pre = pre + b_in_all.astype(jnp.float32)
    hidden = gelu_value(pre).astype(jnp.bfloat16)
    branch = jnp.dot(hidden, w_out_all, preferred_element_type=jnp.float32) + b_out
    output = (features.reshape(rows, chans).astype(jnp.float32) + gamma * branch).astype(
        jnp.bfloat16
    )
    cot_f = cotangent.reshape(rows, chans).astype(jnp.float32)
    d_branch = gamma * cot_f
    d_branch_b = d_branch.astype(jnp.bfloat16)
    d_hidden = lax.dot_general(
        d_branch_b, w_out_all, (((1,), (1,)), ((), ())), preferred_element_type=jnp.float32
    )
    d_pre = d_hidden * gelu_slope(pre)
    d_pre_b = d_pre.astype(jnp.bfloat16)
    d_normed = jnp.dot(d_pre_b, w_in_all, preferred_element_type=jnp.float32)
    term_bi = jnp.sum(d_pre, axis=0) * scale
    term_wo = (
        lax.dot_general(
            hidden, d_branch_b, (((0,), (0,)), ((), ())), preferred_element_type=jnp.float32
        )
        * scale
    )
    term_wi = (
        lax.dot_general(
            d_pre_b, normed_rows, (((0,), (0,)), ((), ())), preferred_element_type=jnp.float32
        )
        * scale
    )
    d_w_in, d_b_in, d_w_out = (
        lax.psum_scatter(term_wi, "space", scatter_dimension=0, tiled=True),
        lax.psum_scatter(term_bi, "space", scatter_dimension=0, tiled=True),
        lax.psum_scatter(term_wo, "space", scatter_dimension=0, tiled=True),
    )
    d_normed = d_normed.reshape(size_x, size_y, size_z, chans)
    term_gain = jnp.sum(d_normed * unit_value, axis=(0, 1, 2)) * scale
    term_bias = jnp.sum(d_normed, axis=(0, 1, 2)) * scale
    scaled = d_normed * ln_gain
    d_mixed = inverse * (
        scaled
        - jnp.mean(scaled, axis=-1, keepdims=True)
        - unit_value * jnp.mean(scaled * unit_value, axis=-1, keepdims=True)
    )
    term_bdw = jnp.sum(d_mixed, axis=(0, 1, 2)) * scale
    d_mixed_b = d_mixed.astype(jnp.bfloat16)
    term_kernel = kernel_terms(padded, d_mixed_b, width) * scale
    term_bout = jnp.sum(d_branch, axis=0) * scale
    term_gamma = jnp.sum(cot_f * branch, axis=0) * scale
    grad_rim = padded_2(d_mixed_b, (("space", 0),), half)
    grad_pad = side_pad(grad_rim, half)
    back = stencil(grad_pad, kernel[::-1, ::-1, ::-1], size_x, size_y, size_z)
    d_x = (cotangent.astype(jnp.float32) + back).astype(jnp.bfloat16)
    bias_units = jnp.zeros((1,), jnp.float32)
    d_kernel, d_b_dw, d_ln_gain, d_ln_bias, d_b_out, d_gamma, bias_sum = lax.psum(
        (term_kernel, term_bdw, term_gain, term_bias, term_bout, term_gamma, bias_units), "space"
    )
    return (
        output.reshape(size_x, size_y, size_z, chans),
        d_x,
        d_kernel,
        d_b_dw,
        d_ln_gain,
        d_ln_bias,
        d_w_in,
        d_b_in,
        d_w_out,
        d_b_out,
        d_gamma,
    )


def solution(mesh):
    in_specs = (
        P(("crop", "space"), None, None, None),
        P(("crop", "space"), None, None, None),
        P(),
        P(),
        P(),
        P(),
        P("space", None),
        P("space"),
        P("space", None),
        P(),
        P(),
    )
    out_specs = (
        P(("crop", "space"), None, None, None),
        P(("crop", "space"), None, None, None),
        P("crop", None, None, None),
        P("crop"),
        P("crop"),
        P("crop"),
        P(("crop", "space"), None),
        P(("crop", "space")),
        P(("crop", "space"), None),
        P("crop"),
        P("crop"),
    )
    return jax.shard_map(
        on_device, mesh=mesh, in_specs=in_specs, out_specs=out_specs, check_vma=False
    )
```

profile of v0, /device:TPU:1, one launch (start us, length us, event | category | flops | bytes accessed | tf_op | source)
XLA Modules:
  0.0 1400.3 jit_solution(2881417611421028055)
XLA Ops:
  13.2 5.1 collective-permute-start.1
  22.2 250.1 %all-reduce.2 = bf16[768]{0:T(1024)(128)(2,1)S(1)} all-reduce(bf16[768]{0:T(1024)(128)(2,1)S(1)} %dynamic-update-slice), channel_id=1, replica_groups=mesh['crop'=4,'space'=128] {'space'}, use_global_device_ids=true, to_apply=%add.2 | all-reduce | flops 768 | bytes 3072
  272.4 83.5 %all-gather = bf16[128,6,192]{2,1,0:T(8,128)(2,1)S(1)} all-gather(bf16[1,6,192]{2,1,0:T(8,128)(2,1)} %bitcast.145), channel_id=1, replica_groups=mesh['crop'=4,'space'=128] {'space'}, dimensions={0}, use_global_device_ids=true | all-gather | bytes 297216 | tf_op jit(solution)/shard_map/all_gather | solution.py:94
  356.2 82.9 %all-gather.1 = bf16[128,6,192]{2,1,0:T(8,128)(2,1)S(1)} all-gather(bf16[1,6,192]{2,1,0:T(8,128)(2,1)S(1)} %bitcast.146), channel_id=1, replica_groups=mesh['crop'=4,'space'=128] {'space'}, dimensions={0}, use_global_device_ids=true | all-gather | bytes 297216 | tf_op jit(solution)/shard_map/all_gather | solution.py:96
  442.8 23.5 %while.93 = (s32[]{:T(128)}, f32[4,8,8,192]{3,2,1,0:T(8,128)S(1)}, bf16[10,14,14,192]{3,2,1,0:T(8,128)(2,1)S(1)}, f32[7,7,7,192]{3,2,1,0:T(8,128)S(1)}, s32[]{:T...) while((s32[]{:T(128)}, f32[4,8,8,192]{3,2,1,0:T(8,128)S(1)}, ...), condition=%wide.region_3.4_spmd, body=%wide.region_0.3_spmd.sunk | while | flops 1032202 | bytes 1775338 | solution.py:50
  471.1 264.9 %fusion.16 = (f32[8,192]{1,0:T(8,128)S(1)}, f32[8,192]{1,0:T(8,128)S(1)}) fusion(f32[768,192]{1,0:T(8,128)S(1)} %convolution_multiply_fusion.1, f32[768,192]{1,0:T(8,128)} %convolution_multiply_fusion), kind=kCustom, calls=%all-reduce-scatter.2 | all-reduce-scatter fusion | flops 393217 | bytes 1193984
  752.2 16.6 %collective-permute-start.44 = (f32[8,192]{1,0:T(8,128)S(1)}, f32[8,192]{1,0:T(8,128)S(1)}, u32[]{:S(2)}, u32[]{:S(2)}) collective-permute-start(f32[8,192]{1,0:T(8,128)S(1)} %get-tuple-element.495), channel_id=1, source_target_pairs={{0,9},{1,10},{2,11},{3,12},{4,13},{5,14},{6,15},{7,16},{8,17},{9,1... | collective-permute-start | bytes 18440
  770.5 15.2 %collective-permute-start.46 = (f32[8,192]{1,0:T(8,128)S(1)}, f32[8,192]{1,0:T(8,128)S(1)}, u32[]{:S(2)}, u32[]{:S(2)}) collective-permute-start(f32[8,192]{1,0:T(8,128)S(1)} %get-tuple-element.495), channel_id=1, source_target_pairs={{0,11},{1,12},{2,13},{3,14},{4,15},{5,16},{6,17},{7,18},{8,19},{9,... | collective-permute-start | bytes 18440
  788.0 6.4 collective-permute-start.48
  794.4 7.5 collective-permute-start.49
  804.2 10.8 collective-permute-start.51
  836.6 166.3 %while.97 = (s32[]{:T(128)}, f32[7,7,7,192]{3,2,1,0:T(8,128)S(1)}, s32[7]{0:T(128)S(1)}, bf16[10,14,14,192]{3,2,1,0:T(8,128)(2,1)S(1)}, f32[4,8,8,192]{3,2,1,0:T...) while((s32[]{:T(128)}, f32[7,7,7,192]{3,2,1,0:T(8,128)S(1)}, ...), condition=%wide.region_22.23_spmd, body=%wide.region_12.22_spmd.sunk | while | flops 1030864 | bytes 1634690 | solution.py:70
  839.2 21.1 %while.100 = (s32[]{:T(128)}, f32[7,7,192]{2,1,0:T(8,128)S(1)}, s32[7]{0:T(128)S(1)}, bf16[4,14,14,192]{3,2,1,0:T(8,128)(2,1)S(1)}, f32[4,8,8,192]{3,2,1,0:T(8,1...) while((s32[]{:T(128)}, f32[7,7,192]{2,1,0:T(8,128)S(1)}, ...), condition=%wide.region_21.21_spmd, body=%wide.region_13.20_spmd.sunk | while | flops 1030859 | bytes 917531 | solution.py:68
  863.0 21.1 %while.100 = (s32[]{:T(128)}, f32[7,7,192]{2,1,0:T(8,128)S(1)}, s32[7]{0:T(128)S(1)}, bf16[4,14,14,192]{3,2,1,0:T(8,128)(2,1)S(1)}, f32[4,8,8,192]{3,2,1,0:T(8,1...) while((s32[]{:T(128)}, f32[7,7,192]{2,1,0:T(8,128)S(1)}, ...), condition=%wide.region_21.21_spmd, body=%wide.region_13.20_spmd.sunk | while | flops 1030859 | bytes 917531 | solution.py:68
  886.7 21.1 %while.100 = (s32[]{:T(128)}, f32[7,7,192]{2,1,0:T(8,128)S(1)}, s32[7]{0:T(128)S(1)}, bf16[4,14,14,192]{3,2,1,0:T(8,128)(2,1)S(1)}, f32[4,8,8,192]{3,2,1,0:T(8,1...) while((s32[]{:T(128)}, f32[7,7,192]{2,1,0:T(8,128)S(1)}, ...), condition=%wide.region_21.21_spmd, body=%wide.region_13.20_spmd.sunk | while | flops 1030859 | bytes 917531 | solution.py:68
  910.5 21.1 %while.100 = (s32[]{:T(128)}, f32[7,7,192]{2,1,0:T(8,128)S(1)}, s32[7]{0:T(128)S(1)}, bf16[4,14,14,192]{3,2,1,0:T(8,128)(2,1)S(1)}, f32[4,8,8,192]{3,2,1,0:T(8,1...) while((s32[]{:T(128)}, f32[7,7,192]{2,1,0:T(8,128)S(1)}, ...), condition=%wide.region_21.21_spmd, body=%wide.region_13.20_spmd.sunk | while | flops 1030859 | bytes 917531 | solution.py:68
  934.3 21.1 %while.100 = (s32[]{:T(128)}, f32[7,7,192]{2,1,0:T(8,128)S(1)}, s32[7]{0:T(128)S(1)}, bf16[4,14,14,192]{3,2,1,0:T(8,128)(2,1)S(1)}, f32[4,8,8,192]{3,2,1,0:T(8,1...) while((s32[]{:T(128)}, f32[7,7,192]{2,1,0:T(8,128)S(1)}, ...), condition=%wide.region_21.21_spmd, body=%wide.region_13.20_spmd.sunk | while | flops 1030859 | bytes 917531 | solution.py:68
  958.0 21.1 %while.100 = (s32[]{:T(128)}, f32[7,7,192]{2,1,0:T(8,128)S(1)}, s32[7]{0:T(128)S(1)}, bf16[4,14,14,192]{3,2,1,0:T(8,128)(2,1)S(1)}, f32[4,8,8,192]{3,2,1,0:T(8,1...) while((s32[]{:T(128)}, f32[7,7,192]{2,1,0:T(8,128)S(1)}, ...), condition=%wide.region_21.21_spmd, body=%wide.region_13.20_spmd.sunk | while | flops 1030859 | bytes 917531 | solution.py:68
  981.8 21.1 %while.100 = (s32[]{:T(128)}, f32[7,7,192]{2,1,0:T(8,128)S(1)}, s32[7]{0:T(128)S(1)}, bf16[4,14,14,192]{3,2,1,0:T(8,128)(2,1)S(1)}, f32[4,8,8,192]{3,2,1,0:T(8,1...) while((s32[]{:T(128)}, f32[7,7,192]{2,1,0:T(8,128)S(1)}, ...), condition=%wide.region_21.21_spmd, body=%wide.region_13.20_spmd.sunk | while | flops 1030859 | bytes 917531 | solution.py:68
  1009.4 5.0 collective-permute-start.10
  1020.6 6.9 collective-permute-start.13
  1027.6 5.9 collective-permute-start.14
  1109.6 28.8 %while.95 = (s32[]{:T(128)}, f32[4,8,8,192]{3,2,1,0:T(8,128)S(1)}, bf16[10,14,14,192]{3,2,1,0:T(8,128)(2,1)S(1)}, f32[7,7,7,192]{3,2,1,0:T(8,128)}, s32[]{:T(128...) while((s32[]{:T(128)}, f32[4,8,8,192]{3,2,1,0:T(8,128)S(1)}, ...), condition=%wide.region_11.12_spmd, body=%wide.region_8.11_spmd.sunk | while | flops 1032202 | bytes 1775338 | solution.py:50
  1139.2 251.9 %all-reduce.8 = (f32[192]{0:T(256)}, f32[192]{0:T(256)}, f32[192]{0:T(256)}, f32[768]{0:T(1024)S(1)}, f32[192]{0:T(256)}, /*index=5*/f32[192]{0:T(256)}) all-reduce(f32[192]{0:T(256)S(1)} %get-tuple-element.531, f32[192]{0:T(256)S(1)} %get-tuple-element.530, ...), channel_id=1, replica_groups=mesh['crop'=4,'space'=128] {'space'}, use_global_device_ids=true, to_apply=%region_25.26 | all-reduce | flops 1728 | bytes 13824 | tf_op jit(solution)/shard_map/psum | solution.py:153
  (783 shorter events, 303.7 us)
Async XLA Ops:
  7.2 1384.5 %all-reduce.12.cloned.1.call-start = ((), (), s32[]{:S(2)}) async-start(), calls=%async_computation | async-start | bytes 802816 | tf_op jit(solution)/shard_map/psum | solution.py:153
  8.2 434.1 %collective-permute-start = (bf16[3,8,8,192]{3,2,1,0:T(8,128)(2,1)S(1)}, bf16[3,8,8,192]{3,2,1,0:T(8,128)(2,1)S(1)}, u32[]{:S(2)}, u32[]{:S(2)}) collective-permute-start(bf16[3,8,8,192]{3,2,1,0:T(8,128)(2,1)S(1)} %get-tuple-element.520), channel_id=1, source_target_pairs={{0,1},{1,2},{2,3},{3,4},{4,5},{5,6},{6,7},{7,8},{8,9},{9,10},{10,1... | collective-permute-start | bytes 221192 | tf_op jit(solution)/shard_map/ppermute | solution.py:17
  13.2 429.2 %collective-permute-start.1 = (bf16[3,8,8,192]{3,2,1,0:T(8,128)(2,1)S(1)}, bf16[3,8,8,192]{3,2,1,0:T(8,128)(2,1)S(1)}, u32[]{:S(2)}, u32[]{:S(2)}) collective-permute-start(bf16[3,8,8,192]{3,2,1,0:T(8,128)(2,1)S(1)} %get-tuple-element.521), channel_id=1, source_target_pairs={{1,0},{2,1},{3,2},{4,3},{5,4},{6,5},{7,6},{8,7},{9,8},{10,9},{11,1... | collective-permute-start | bytes 221192 | tf_op jit(solution)/shard_map/ppermute | solution.py:18
  746.7 22.1 %collective-permute-start.40 = (f32[8,192]{1,0:T(8,128)S(1)}, f32[8,192]{1,0:T(8,128)S(1)}, u32[]{:S(2)}, u32[]{:S(2)}) collective-permute-start(f32[8,192]{1,0:T(8,128)S(1)} %get-tuple-element.495), channel_id=1, source_target_pairs={{0,5},{1,6},{2,7},{3,8},{4,9},{5,10},{6,11},{7,12},{8,13},{9,14},{... | collective-permute-start | bytes 18440
  748.0 22.5 %collective-permute-start.41 = (f32[8,192]{1,0:T(8,128)S(1)}, f32[8,192]{1,0:T(8,128)S(1)}, u32[]{:S(2)}, u32[]{:S(2)}) collective-permute-start(f32[8,192]{1,0:T(8,128)S(1)} %get-tuple-element.495), channel_id=1, source_target_pairs={{0,6},{1,7},{2,8},{3,9},{4,10},{5,11},{6,12},{7,13},{8,14},{9,15},... | collective-permute-start | bytes 18440
  749.3 36.4 %collective-permute-start.42 = (f32[8,192]{1,0:T(8,128)S(1)}, f32[8,192]{1,0:T(8,128)S(1)}, u32[]{:S(2)}, u32[]{:S(2)}) collective-permute-start(f32[8,192]{1,0:T(8,128)S(1)} %get-tuple-element.495), channel_id=1, source_target_pairs={{0,7},{1,8},{2,9},{3,10},{4,11},{5,12},{6,13},{7,14},{8,15},{9,16}... | collective-permute-start | bytes 18440
  750.9 37.1 %collective-permute-start.43 = (f32[8,192]{1,0:T(8,128)S(1)}, f32[8,192]{1,0:T(8,128)S(1)}, u32[]{:S(2)}, u32[]{:S(2)}) collective-permute-start(f32[8,192]{1,0:T(8,128)S(1)} %get-tuple-element.495), channel_id=1, source_target_pairs={{0,8},{1,9},{2,10},{3,11},{4,12},{5,13},{6,14},{7,15},{8,16},{9,17... | collective-permute-start | bytes 18440
  752.2 42.2 %collective-permute-start.44 = (f32[8,192]{1,0:T(8,128)S(1)}, f32[8,192]{1,0:T(8,128)S(1)}, u32[]{:S(2)}, u32[]{:S(2)}) collective-permute-start(f32[8,192]{1,0:T(8,128)S(1)} %get-tuple-element.495), channel_id=1, source_target_pairs={{0,9},{1,10},{2,11},{3,12},{4,13},{5,14},{6,15},{7,16},{8,17},{9,1... | collective-permute-start | bytes 18440
  768.8 33.2 %collective-permute-start.45 = (f32[8,192]{1,0:T(8,128)S(1)}, f32[8,192]{1,0:T(8,128)S(1)}, u32[]{:S(2)}, u32[]{:S(2)}) collective-permute-start(f32[8,192]{1,0:T(8,128)S(1)} %get-tuple-element.495), channel_id=1, source_target_pairs={{0,10},{1,11},{2,12},{3,13},{4,14},{5,15},{6,16},{7,17},{8,18},{9,... | collective-permute-start | bytes 18440
  770.5 33.7 %collective-permute-start.46 = (f32[8,192]{1,0:T(8,128)S(1)}, f32[8,192]{1,0:T(8,128)S(1)}, u32[]{:S(2)}, u32[]{:S(2)}) collective-permute-start(f32[8,192]{1,0:T(8,128)S(1)} %get-tuple-element.495), channel_id=1, source_target_pairs={{0,11},{1,12},{2,13},{3,14},{4,15},{5,16},{6,17},{7,18},{8,19},{9,... | collective-permute-start | bytes 18440
  785.7 29.3 %collective-permute-start.47 = (f32[8,192]{1,0:T(8,128)S(1)}, f32[8,192]{1,0:T(8,128)S(1)}, u32[]{:S(2)}, u32[]{:S(2)}) collective-permute-start(f32[8,192]{1,0:T(8,128)S(1)} %get-tuple-element.495), channel_id=1, source_target_pairs={{0,12},{1,13},{2,14},{3,15},{4,16},{5,17},{6,18},{7,19},{8,20},{9,... | collective-permute-start | bytes 18440
  788.0 28.9 %collective-permute-start.48 = (f32[8,192]{1,0:T(8,128)S(1)}, f32[8,192]{1,0:T(8,128)S(1)}, u32[]{:S(2)}, u32[]{:S(2)}) collective-permute-start(f32[8,192]{1,0:T(8,128)S(1)} %get-tuple-element.495), channel_id=1, source_target_pairs={{0,13},{1,14},{2,15},{3,16},{4,17},{5,18},{6,19},{7,20},{8,21},{9,... | collective-permute-start | bytes 18440
  794.4 23.9 %collective-permute-start.49 = (f32[8,192]{1,0:T(8,128)S(1)}, f32[8,192]{1,0:T(8,128)S(1)}, u32[]{:S(2)}, u32[]{:S(2)}) collective-permute-start(f32[8,192]{1,0:T(8,128)S(1)} %get-tuple-element.495), channel_id=1, source_target_pairs={{0,14},{1,15},{2,16},{3,17},{4,18},{5,19},{6,20},{7,21},{8,22},{9,... | collective-permute-start | bytes 18440
  830.0 173.0 %collective-permute-start.58 = (f32[8,192]{1,0:T(8,128)S(1)}, f32[8,192]{1,0:T(8,128)S(1)}, u32[]{:S(2)}, u32[]{:S(2)}) collective-permute-start(f32[8,192]{1,0:T(8,128)S(1)} %get-tuple-element.495), channel_id=1, source_target_pairs={{0,23},{1,24},{2,25},{3,26},{4,27},{5,28},{6,29},{7,30},{8,31},{9,... | collective-permute-start | bytes 18440
  831.3 173.2 %collective-permute-start.59 = (f32[8,192]{1,0:T(8,128)S(1)}, f32[8,192]{1,0:T(8,128)S(1)}, u32[]{:S(2)}, u32[]{:S(2)}) collective-permute-start(f32[8,192]{1,0:T(8,128)S(1)} %get-tuple-element.495), channel_id=1, source_target_pairs={{0,24},{1,25},{2,26},{3,27},{4,28},{5,29},{6,30},{7,31},{8,32},{9,... | collective-permute-start | bytes 18440
  832.6 174.2 %collective-permute-start.60 = (f32[8,192]{1,0:T(8,128)S(1)}, f32[8,192]{1,0:T(8,128)S(1)}, u32[]{:S(2)}, u32[]{:S(2)}) collective-permute-start(f32[8,192]{1,0:T(8,128)S(1)} %get-tuple-element.495), channel_id=1, source_target_pairs={{0,25},{1,26},{2,27},{3,28},{4,29},{5,30},{6,31},{7,32},{8,33},{9,... | collective-permute-start | bytes 18440
  833.9 174.2 %collective-permute-start.61 = (f32[8,192]{1,0:T(8,128)S(1)}, f32[8,192]{1,0:T(8,128)S(1)}, u32[]{:S(2)}, u32[]{:S(2)}) collective-permute-start(f32[8,192]{1,0:T(8,128)S(1)} %get-tuple-element.495), channel_id=1, source_target_pairs={{0,26},{1,27},{2,28},{3,29},{4,30},{5,31},{6,32},{7,33},{8,34},{9,... | collective-permute-start | bytes 18440
  835.2 174.2 %collective-permute-start.62 = (f32[8,192]{1,0:T(8,128)S(1)}, f32[8,192]{1,0:T(8,128)S(1)}, u32[]{:S(2)}, u32[]{:S(2)}) collective-permute-start(f32[8,192]{1,0:T(8,128)S(1)} %get-tuple-element.495), channel_id=1, source_target_pairs={{0,27},{1,28},{2,29},{3,30},{4,31},{5,32},{6,33},{7,34},{8,35},{9,... | collective-permute-start | bytes 18440
  1008.1 19.4 %collective-permute-start.66 = (f32[8,192]{1,0:T(8,128)S(1)}, f32[8,192]{1,0:T(8,128)S(1)}, u32[]{:S(2)}, u32[]{:S(2)}) collective-permute-start(f32[8,192]{1,0:T(8,128)S(1)} %get-tuple-element.495), channel_id=1, source_target_pairs={{0,31},{1,32},{2,33},{3,34},{4,35},{5,36},{6,37},{7,38},{8,39},{9,... | collective-permute-start | bytes 18440
  1009.4 24.1 %collective-permute-start.10 = (f32[8,192]{1,0:T(8,128)S(1)}, f32[8,192]{1,0:T(8,128)S(1)}, u32[]{:S(2)}, u32[]{:S(2)}) collective-permute-start(f32[8,192]{1,0:T(8,128)S(1)} %get-tuple-element.494), channel_id=1, source_target_pairs={{0,7},{1,8},{2,9},{3,10},{4,11},{5,12},{6,13},{7,14},{8,15},{9,16}... | collective-permute-start | bytes 18440
  1015.3 20.0 %collective-permute-start.11 = (f32[8,192]{1,0:T(8,128)S(1)}, f32[8,192]{1,0:T(8,128)S(1)}, u32[]{:S(2)}, u32[]{:S(2)}) collective-permute-start(f32[8,192]{1,0:T(8,128)S(1)} %get-tuple-element.494), channel_id=1, source_target_pairs={{0,8},{1,9},{2,10},{3,11},{4,12},{5,13},{6,14},{7,15},{8,16},{9,17... | collective-permute-start | bytes 18440
  1018.8 20.9 %collective-permute-start.12 = (f32[8,192]{1,0:T(8,128)S(1)}, f32[8,192]{1,0:T(8,128)S(1)}, u32[]{:S(2)}, u32[]{:S(2)}) collective-permute-start(f32[8,192]{1,0:T(8,128)S(1)} %get-tuple-element.494), channel_id=1, source_target_pairs={{0,9},{1,10},{2,11},{3,12},{4,13},{5,14},{6,15},{7,16},{8,17},{9,1... | collective-permute-start | bytes 18440
  1020.6 22.9 %collective-permute-start.13 = (f32[8,192]{1,0:T(8,128)S(1)}, f32[8,192]{1,0:T(8,128)S(1)}, u32[]{:S(2)}, u32[]{:S(2)}) collective-permute-start(f32[8,192]{1,0:T(8,128)S(1)} %get-tuple-element.494), channel_id=1, source_target_pairs={{0,10},{1,11},{2,12},{3,13},{4,14},{5,15},{6,16},{7,17},{8,18},{9,... | collective-permute-start | bytes 18440
  1076.6 19.4 %collective-permute-start.4 = (f32[8,192]{1,0:T(8,128)S(1)}, f32[8,192]{1,0:T(8,128)S(1)}, u32[]{:S(2)}, u32[]{:S(2)}) collective-permute-start(f32[8,192]{1,0:T(8,128)S(1)} %get-tuple-element.494), channel_id=1, source_target_pairs={{0,1},{1,2},{2,3},{3,4},{4,5},{5,6},{6,7},{7,8},{8,9},{9,10},{10,1... | collective-permute-start | bytes 18440
  (112 other events, 4106.9 us)
Sparse Core Ops, SparseCore 0:
  1050.7 316.2 all-reduce.11
where the time goes:
time: 1410 us; the launch traced here: 1400 us
  blocking collectives  933 us (66%)
  starting transfers between devices  201 us (14%)
  loops' own time  111 us (8%)
  other arithmetic  67.5 us (5%)
  local copies, waits for them, and re-layouts  62.9 us (4%)
  between operations  18.3 us (1%)
    unnamed x2, blocking collectives  515 us
    psum x1, blocking collectives, on_device(): lax.psum((term_kernel, term_bdw, term_gain, term_bias, term_bout, term_ga...  252 us
    unnamed x64, starting transfers between devices  185 us
    another operation x7, loops' own time, kernel_over_x(): return lax.map(kernel_over_y, jnp.arange(width, dtype=jnp.int32))  94.8 us
    all_gather x1, blocking collectives, on_device(): lax.all_gather(w_in_t, 'space', axis=0, tiled=True)  83.5 us
    all_gather x1, blocking collectives, on_device(): lax.all_gather(w_out, 'space', axis=0, tiled=True)  82.9 us
    add x98, other arithmetic, stencil_over_y(): inner = inner + window.astype(jnp.float32) * taps_y[along_z]  41.2 us
    dynamic_slice x56, local copies, waits for them, and re-layouts, kernel_terms(): return lax.map(kernel_over_x, jnp.arange(width, dtype=jnp.int32))  34.1 us
  transfers between devices with their start and end apart: 69, of which 1 were waited for; matrix products, arithmetic and copies ran while one was open for 7% of the time, Pallas kernels for 0%

commit v1 on v0

v1 whole, which is shorter than its diff:
```python
import numpy as np
import jax
import jax.numpy as jnp
import ml_dtypes
from jax import lax
from jax.experimental import pallas as pl
from jax.experimental.pallas import tpu as pltpu
from jax.sharding import PartitionSpec as P

root_half = 0.7071067811865476
inv_root_tau = 0.3989422804014327
MESH = pl.DeviceIdType.MESH
F32 = jnp.float32
BF = jnp.bfloat16

NX, NZ, NS = 4, 16, 128
C = 192
W = 7
G = 8
SX = 4
CELLS = SX * G * G
N = 11
NF = 64
UNITS = 6
LANES = 512
GROUPS = 7
TILES = 2 * GROUPS


def split_np(m):
    high = m.astype(ml_dtypes.bfloat16)
    low = (m - high.astype(np.float64)).astype(ml_dtypes.bfloat16)
    return high, low


def transforms():
    seen, reps = set(), []
    for u in range(N):
        for v in range(N):
            if (u, v) in seen:
                continue
            reps.append((u, v))
            seen.add((u, v))
            seen.add(((-u) % N, (-v) % N))
    u = np.array([r[0] for r in reps])[:, None]
    v = np.array([r[1] for r in reps])[:, None]
    weight = np.where((u == 0) & (v == 0), 1.0, 2.0) / N**2
    n = len(reps)

    def table(pos_j, pos_k, live, sign):
        angle = 2 * np.pi / N * (u * pos_j[None] + v * pos_k[None])
        out = np.zeros((2 * NF, len(pos_j)))
        out[:n] = np.cos(angle) * live
        out[NF : NF + n] = sign * np.sin(angle) * live
        return out

    scale = np.zeros((2 * NF, 1))
    scale[:n] = weight
    scale[NF : NF + n] = weight
    cell = np.arange(G * G)
    tap = np.arange(8 * W)
    live = ((tap % 8) < W)[None]
    fwd = table(cell // G, cell % G, 1.0, -1.0)
    inv = (fwd * scale).T
    ker = table(tap // 8 - 3, tap % 8 - 3, live, 1.0)
    lag = (table(tap // 8 - 3, tap % 8 - 3, live, -1.0) * scale).T
    fm = np.concatenate(split_np(fwd), axis=0)
    return fm, np.stack(split_np(ker)), np.stack(split_np(inv)), np.stack(split_np(lag))


def dot(a, b):
    return jnp.dot(a, b, preferred_element_type=F32)


def dot_nt(a, b):
    return lax.dot_general(a, b, (((1,), (1,)), ((), ())), preferred_element_type=F32)


def dot_tn(a, b):
    return lax.dot_general(a, b, (((0,), (0,)), ((), ())), preferred_element_type=F32)


def halves(value):
    high = value.astype(BF)
    return high, (value - high.astype(F32)).astype(BF)


def dot3(m, value):
    high, low = halves(value)
    return dot(m[0], high) + dot(m[1], high) + dot(m[0], low)


def kernel_body(
    x_ref, cot_ref, ker_ref, bdw_ref, gain_ref, bias_ref, blk_ref, bout_ref, gamma_ref,
    fm_ref, km_ref, im_ref, lm_ref,
    out_ref, dx_ref, dker_ref, vec_ref, dwi_ref, dwo_ref, dbi_ref,
    halo_x, halo_d, wall, swall, r1, t1, t1b, r2, t2, t2b, r3,
    kpad, kf, xf, df, yf, gf, mixed, na, dba, branch, dnorm, dmb,
    pay, payb, rx, zt, ztb, rz, agz, fin,
    s_halo, q_halo, s_ga, q_ga, s_gb, q_gb, s_gc, q_gc, s_hd, q_hd,
    s_rc, q_rc, s_rb, q_rb, s_ra, q_ra, s_px, q_px, s_pz, q_pz, s_az, q_az, s_ax, q_ax,
):
    scale = float(NS * CELLS) ** (-0.5)
    s = lax.axis_index("space")
    core = lax.rem(s, 2)
    z = lax.rem(s // 2, NZ)
    x = s // (2 * NZ)

    def place(px, pz, pc):
        return {"space": (px * NZ + pz) * 2 + pc}

    def at_z(d):
        return place(x, lax.rem(z + d + NZ, NZ), core)

    def at_x(d):
        return place(lax.rem(x + d + NX, NX), z, core)

    def at_xc(k):
        return place(lax.rem(x + k % NX, NX), z, core if k < NX else 1 - core)

    partner = place(x, z, 1 - core)
    right = {"space": lax.rem(s + 1, NS)}
    left = {"space": lax.rem(s + NS - 1, NS)}

    def copy(src, dst, ssem, rsem, dev):
        return pltpu.make_async_remote_copy(
            src_ref=src, dst_ref=dst, send_sem=ssem, recv_sem=rsem, device_id=dev, device_id_type=MESH
        )

    pending = []

    def launch(copies):
        for c in copies:
            c.start()
        pending.extend(copies)
        return copies

    def arrive(copies):
        for c in copies:
            c.wait_recv()

    barrier = pltpu.get_barrier_semaphore()
    peers = [at_z(d) for d in range(1, NZ)] + [at_xc(k) for k in range(1, 2 * NX)] + [left, right]
    for dev in peers:
        pl.semaphore_signal(barrier, inc=1, device_id=dev, device_id_type=MESH)
    pl.semaphore_wait(barrier, len(peers))

    halo = launch([
        copy(x_ref.at[pl.ds(64, 192)], halo_x.at[0], s_halo.at[0], q_halo.at[0], right),
        copy(x_ref.at[pl.ds(0, 192)], halo_x.at[1], s_halo.at[1], q_halo.at[1], left),
    ])
    gather_a = launch([
        copy(blk_ref, wall.at[0, 0, d], s_ga.at[d - 1], q_ga.at[d - 1], at_z(d)) for d in range(1, NZ)
    ])
    wall[0, 0, 0] = blk_ref[...]

    kpad[...] = jnp.zeros_like(kpad)
    for a in range(W):
        for b in range(W):
            kpad[a, 8 * b : 8 * b + W, :] = ker_ref[a, b]

    def transform(rows):
        both = dot(fm_ref[...], rows)
        return both[: 2 * NF] + both[2 * NF :]

    km = (km_ref[0], km_ref[1])

    def ker_step(a, carry):
        kf[a] = dot3(km, kpad[a])
        return carry

    lax.fori_loop(0, W, ker_step, 0)
    for p in range(SX):
        xf[3 + p] = transform(x_ref[64 * p : 64 * p + 64, :])

    arrive(gather_a)
    gather_b = launch([
        copy(wall.at[0, 0], wall.at[0, d], s_gb.at[d - 1], q_gb.at[d - 1], at_x(d)) for d in range(1, NX)
    ])

    arrive(halo)
    has_left = (s > 0).astype(F32)
    has_right = (s < NS - 1).astype(F32)
    for p in range(3):
        xf[p] = transform(halo_x[0, 64 * p : 64 * p + 64, :]) * has_left
        xf[7 + p] = transform(halo_x[1, 64 * p : 64 * p + 64, :]) * has_right

    def forward_step(g, carry):
        top, low = pl.ds(pl.multiple_of(8 * g, 8), 8), pl.ds(pl.multiple_of(8 * g + NF, 8), 8)
        re = jnp.zeros((SX, 8, C), F32)
        im = jnp.zeros((SX, 8, C), F32)
        for a in range(W):
            kr, ki = kf[a, top, :], kf[a, low, :]
            xr, xi = xf[a : a + SX, top, :], xf[a : a + SX, low, :]
            re = re + kr * xr - ki * xi
            im = im + kr * xi + ki * xr
        yf[:, top, :] = re
        yf[:, low, :] = im
        return carry

    lax.fori_loop(0, NF // 8, forward_step, 0)
    inv = (im_ref[0], im_ref[1])
    for p in range(SX):
        mixed[64 * p : 64 * p + 64, :] = dot3(inv, yf[p]) + bdw_ref[...]

    arrive(gather_b)
    gather_c = launch([copy(wall.at[0], wall.at[1], s_gc.at[0], q_gc.at[0], partner)])

    mix = mixed[...]
    centred = mix - jnp.mean(mix, axis=-1, keepdims=True)
    inverse = lax.rsqrt(jnp.mean(centred * centred, axis=-1, keepdims=True) + 1e-06)
    unit = centred * inverse
    mixed[...] = unit
    lane = lax.broadcasted_iota(jnp.int32, (CELLS, 128), 1)
    na[:, 128:256] = jnp.where(lane == C - 128, 1.0, 0.0).astype(BF)
    na[:, 0:C] = (unit * gain_ref[...] + bias_ref[...]).astype(BF)
    dba[:, 128:256] = jnp.zeros((CELLS, 128), BF)
    dba[:, 0:C] = (gamma_ref[...] * cot_ref[...].astype(F32)).astype(BF)
    branch[...] = jnp.zeros_like(branch)
    dnorm[...] = jnp.zeros_like(dnorm)

    def units(dc):
        def chunk(i, carry):
            two = pl.ds(2 * i, 2)
            rows = wall[dc, two].astype(F32).reshape(256, LANES).astype(BF)
            win, wout = rows[:, 0:256], rows[:, 256:512]
            normed, db = na[...], dba[...]
            pre = dot_nt(normed, win)
            half_erf = 0.5 * (1.0 + lax.erf(pre * root_half))
            hidden = (pre * half_erf).astype(BF)
            slope = half_erf + pre * jnp.exp(-0.5 * pre * pre) * inv_root_tau
            branch[...] += dot(hidden, wout)
            d_pre = (dot_nt(db, wout) * slope).astype(BF)
            dnorm[...] += dot(d_pre, win)
            dwi = (dot_tn(d_pre, normed) * scale).reshape(2, NZ, 8, 256)
            dwo = (dot_tn(hidden, db) * scale).reshape(2, NZ, 8, 256)
            if dc == 0:
                t1[two, :, :, 0:256] = dwi
                t1[two, :, :, 256:512] = dwo
            else:
                swall[two, :, :, 0:256] = dwi.astype(BF)
                swall[two, :, :, 256:512] = dwo.astype(BF)
            return carry

        lax.fori_loop(0, 2, chunk, 0)

    units(0)
    arrive(gather_c)
    units(1)
    scatter_c = launch([copy(swall, r1, s_rc.at[0], q_rc.at[0], partner)])

    cot = cot_ref[...].astype(F32)
    full = branch[:, 0:C] + bout_ref[...]
    out_ref[...] = (x_ref[...].astype(F32) + gamma_ref[...] * full).astype(BF)
    v_gamma = jnp.sum(cot * full, axis=0, keepdims=True)
    v_bout = jnp.sum(gamma_ref[...] * cot, axis=0, keepdims=True)

    dn = dnorm[:, 0:C]
    unit2 = mixed[...]
    v_gain = jnp.sum(dn * unit2, axis=0, keepdims=True)
    v_bias = jnp.sum(dn, axis=0, keepdims=True)
    scaled = dn * gain_ref[...]
    d_mixed = inverse * (
        scaled
        - jnp.mean(scaled, axis=-1, keepdims=True)
        - unit2 * jnp.mean(scaled * unit2, axis=-1, keepdims=True)
    )
    v_bdw = jnp.sum(d_mixed, axis=0, keepdims=True)
    dmb[...] = d_mixed.astype(BF)
    halo2 = launch([
        copy(dmb.at[pl.ds(64, 192)], halo_d.at[0], s_hd.at[0], q_hd.at[0], right),
        copy(dmb.at[pl.ds(0, 192)], halo_d.at[1], s_hd.at[1], q_hd.at[1], left),
    ])
    for p in range(SX):
        df[3 + p] = transform(dmb[64 * p : 64 * p + 64, :])

    def grad_step(g, carry):
        top, low = pl.ds(pl.multiple_of(8 * g, 8), 8), pl.ds(pl.multiple_of(8 * g + NF, 8), 8)
        dr, di = df[3 : 3 + SX, top, :], df[3 : 3 + SX, low, :]
        for a in range(W):
            xr, xi = xf[a : a + SX, top, :], xf[a : a + SX, low, :]
            gf[a, top, :] = jnp.sum(dr * xr + di * xi, axis=0)
            gf[a, low, :] = jnp.sum(dr * xi - di * xr, axis=0)
        return carry

    lax.fori_loop(0, NF // 8, grad_step, 0)
    lag = (lm_ref[0], lm_ref[1])
    pay[...] = jnp.zeros_like(pay)
    vectors = [v_bdw, v_gain, v_bias, v_bout, v_gamma]
    for a in range(W):
        taps = dot3(lag, gf[a]) * scale
        for b in range(W):
            group = a * W + b
            block = taps[8 * b : 8 * b + 8, :]
            q, t = group // GROUPS, 2 * (group % GROUPS)
            pay[q, t] = block[:, 0:128]
            pay[q, t + 1, :, 0 : C - 128] = block[:, 128:C]
    for i, v in enumerate(vectors):
        pay[0, 2 * i, W : W + 1, :] = v[:, 0:128] * scale
        pay[0, 2 * i + 1, W : W + 1, 0 : C - 128] = v[:, 128:C] * scale
    payb[...] = pay[...].astype(BF)

    def chunk_of(k):
        px = lax.rem(x + k % NX, NX)
        pc = core if k < NX else 1 - core
        return pc * NX + px

    own = chunk_of(0)
    sum_x = launch([
        copy(payb.at[chunk_of(k)], rx.at[k - 1], s_px.at[k - 1], q_px.at[k - 1], at_xc(k))
        for k in range(1, 2 * NX)
    ])

    arrive(scatter_c)

    def add_core(i, carry):
        total = t1[i] + r1[i].astype(F32)
        t1[i] = total
        t1b[i] = total.astype(BF)
        return carry

    lax.fori_loop(0, NX, add_core, 0)
    scatter_b = launch([
        copy(t1b.at[d], r2.at[d - 1], s_rb.at[d - 1], q_rb.at[d - 1], at_x(-d)) for d in range(1, NX)
    ])

    arrive(halo2)
    for p in range(3):
        df[p] = transform(halo_d[0, 64 * p : 64 * p + 64, :]) * has_left
        df[7 + p] = transform(halo_d[1, 64 * p : 64 * p + 64, :]) * has_right

    arrive(sum_x)
    total = pay[own]
    for k in range(2 * NX - 1):
        total = total + rx[k].astype(F32)
    zt[...] = total
    ztb[...] = total.astype(BF)
    sum_z = launch([
        copy(ztb.at[lax.rem(z + d, NZ)], rz.at[d - 1], s_pz.at[d - 1], q_pz.at[d - 1], at_z(d))
        for d in range(1, NZ)
    ])

    def back_step(g, carry):
        top, low = pl.ds(pl.multiple_of(8 * g, 8), 8), pl.ds(pl.multiple_of(8 * g + NF, 8), 8)
        re = jnp.zeros((SX, 8, C), F32)
        im = jnp.zeros((SX, 8, C), F32)
        for a in range(W):
            kr, ki = kf[W - 1 - a, top, :], kf[W - 1 - a, low, :]
            dr, di = df[a : a + SX, top, :], df[a : a + SX, low, :]
            re = re + kr * dr + ki * di
            im = im + kr * di - ki * dr
        yf[:, top, :] = re
        yf[:, low, :] = im
        return carry

    lax.fori_loop(0, NF // 8, back_step, 0)

    arrive(scatter_b)
    t2v = t1[0]
    for d in range(NX - 1):
        t2v = t2v + r2[d].astype(F32)
    t2[...] = t2v
    t2b[...] = t2v.astype(BF)
    scatter_a = launch([
        copy(t2b.at[d], r3.at[d - 1], s_ra.at[d - 1], q_ra.at[d - 1], at_z(-d)) for d in range(1, NZ)
    ])

    arrive(sum_z)
    tile = zt[z]
    for d in range(NZ - 1):
        tile = tile + rz[d].astype(F32)
    agz[z] = tile.astype(BF)
    gather_z = launch([
        copy(agz.at[z], agz.at[z], s_az.at[d - 1], q_az.at[d - 1], at_z(d)) for d in range(1, NZ)
    ])

    for p in range(SX):
        rows = slice(64 * p, 64 * p + 64)
        dx_ref[rows, :] = (cot_ref[rows, :].astype(F32) + dot3(inv, yf[p])).astype(BF)

    arrive(gather_z)
    fin[own] = agz[...]
    gather_x = launch([
        copy(agz, fin.at[own], s_ax.at[k - 1], q_ax.at[k - 1], at_xc(k)) for k in range(1, 2 * NX)
    ])

    arrive(scatter_a)
    mine = t2[0]
    for d in range(NZ - 1):
        mine = mine + r3[d].astype(F32)
    dwi_ref[...] = mine[0:UNITS, 0:C]
    dwo_ref[...] = mine[0:UNITS, 256 : 256 + C]
    row = lax.broadcasted_iota(jnp.int32, (8, 128), 0)
    col = lax.broadcasted_iota(jnp.int32, (8, 128), 1)
    bias_col = jnp.broadcast_to(mine[:, C : C + 1], (8, 128))
    dbi_ref[...] = jnp.sum(jnp.where(row == col, bias_col, 0.0), axis=0, keepdims=True)

    arrive(gather_x)
    for group in range(W * W):
        q, t = group // GROUPS, 2 * (group % GROUPS)
        first, second = fin[q, t].astype(F32), fin[q, t + 1].astype(F32)
        dker_ref[group // W, group % W, :, 0:128] = first[0:W]
        dker_ref[group // W, group % W, :, 128:C] = second[0:W, 0 : C - 128]
        if group < 5:
            vec_ref[group : group + 1, 0:128] = first[W : W + 1]
            vec_ref[group : group + 1, 128:C] = second[W : W + 1, 0 : C - 128]

    for c in pending:
        c.wait_send()


def on_device(
    features, cotangent, kernel, b_dw, ln_gain, ln_bias, w_in_t, b_in, w_out, b_out, gamma
):
    block = jnp.concatenate(
        [
            jnp.pad(jnp.concatenate([w_in_t, b_in[:, None]], axis=1), ((0, 2), (0, 255 - C))),
            jnp.pad(w_out, ((0, 2), (0, 256 - C))),
        ],
        axis=1,
    )
    fm, km, im, lm = (jnp.asarray(m) for m in transforms())
    vm = pl.BlockSpec(memory_space=pltpu.VMEM)
    dma = pltpu.SemaphoreType.DMA
    counts = [2, NZ - 1, NX - 1, 1, 2, 1, NX - 1, NZ - 1, 2 * NX - 1, NZ - 1, NZ - 1, 2 * NX - 1]
    sems = [dma((n,)) for n in counts for _ in range(2)]
    scratch = [
        pltpu.VMEM((2, 192, C), BF),
        pltpu.VMEM((2, 192, C), BF),
        pltpu.VMEM((2, NX, NZ, 8, LANES), BF),
        pltpu.VMEM((NX, NZ, 8, LANES), BF),
        pltpu.VMEM((NX, NZ, 8, LANES), BF),
        pltpu.VMEM((NX, NZ, 8, LANES), F32),
        pltpu.VMEM((NX, NZ, 8, LANES), BF),
        pltpu.VMEM((NX - 1, NZ, 8, LANES), BF),
        pltpu.VMEM((NZ, 8, LANES), F32),
        pltpu.VMEM((NZ, 8, LANES), BF),
        pltpu.VMEM((NZ - 1, 8, LANES), BF),
        pltpu.VMEM((W, 8 * W, C), F32),
        pltpu.VMEM((W, 2 * NF, C), F32),
        pltpu.VMEM((SX + 6, 2 * NF, C), F32),
        pltpu.VMEM((SX + 6, 2 * NF, C), F32),
        pltpu.VMEM((SX, 2 * NF, C), F32),
        pltpu.VMEM((W, 2 * NF, C), F32),
        pltpu.VMEM((CELLS, C), F32),
        pltpu.VMEM((CELLS, 256), BF),
        pltpu.VMEM((CELLS, 256), BF),
        pltpu.VMEM((CELLS, 256), F32),
        pltpu.VMEM((CELLS, 256), F32),
        pltpu.VMEM((CELLS, C), BF),
        pltpu.VMEM((2 * NX, NZ, 8, 128), F32),
        pltpu.VMEM((2 * NX, NZ, 8, 128), BF),
        pltpu.VMEM((2 * NX - 1, NZ, 8, 128), BF),
        pltpu.VMEM((NZ, 8, 128), F32),
        pltpu.VMEM((NZ, 8, 128), BF),
        pltpu.VMEM((NZ - 1, 8, 128), BF),
        pltpu.VMEM((NZ, 8, 128), BF),
        pltpu.VMEM((2 * NX, NZ, 8, 128), BF),
    ]
    out, dx, dker, vec, dwi, dwo, dbi = pl.pallas_call(
        kernel_body,
        out_shape=(
            jax.ShapeDtypeStruct((CELLS, C), BF),
            jax.ShapeDtypeStruct((CELLS, C), BF),
            jax.ShapeDtypeStruct((W, W, W, C), F32),
            jax.ShapeDtypeStruct((8, C), F32),
            jax.ShapeDtypeStruct((UNITS, C), F32),
            jax.ShapeDtypeStruct((UNITS, C), F32),
            jax.ShapeDtypeStruct((1, 128), F32),
        ),
        in_specs=[vm] * 13,
        out_specs=(vm,) * 7,
        scratch_shapes=scratch + sems,
        compiler_params=pltpu.CompilerParams(
            collective_id=0, has_side_effects=True, vmem_limit_bytes=48 * 1024 * 1024
        ),
    )(
        features.reshape(CELLS, C), cotangent.reshape(CELLS, C), kernel,
        b_dw.reshape(1, C), ln_gain.reshape(1, C), ln_bias.reshape(1, C), block,
        b_out.reshape(1, C), gamma.reshape(1, C), fm, km, im, lm,
    )
    shape = features.shape
    return (
        out.reshape(shape), dx.reshape(shape), dker,
        vec[0], vec[1], vec[2], dwi, dbi[0, 0:UNITS], dwo, vec[3], vec[4],
    )


def solution(mesh):
    cells = P(("crop", "space"), None, None, None)
    rows = P(("crop", "space"), None)
    in_specs = (
        cells, cells, P(), P(), P(), P(), P("space", None), P("space"), P("space", None), P(), P(),
    )
    out_specs = (
        cells, cells, P("crop", None, None, None), P("crop"), P("crop"), P("crop"),
        rows, P(("crop", "space")), rows, P("crop"), P("crop"),
    )
    return jax.shard_map(
        on_device, mesh=mesh, in_specs=in_specs, out_specs=out_specs, check_vma=False
    )
```

time: 1410 us -> 82.9 us (0.06)
  blocking collectives: 933 us -> 0 us
  starting transfers between devices: 201 us -> 0 us
  loops' own time: 111 us -> 0 us
  Pallas kernels: 0 us -> 69.9 us
  other arithmetic: 67.5 us -> 1.5 us
  local copies, waits for them, and re-layouts: 62.9 us -> 10.4 us
  between operations: 18.3 us -> 0.73 us
    unnamed x2 -> x0, blocking collectives: 515 us -> none
    psum x1 -> x0, blocking collectives: 252 us -> none  [on_device(): lax.psum((term_kernel, term_bdw, term_gain, term_bias, term_bout, term_ga...]
    unnamed x64 -> x0, starting transfers between devices: 185 us -> none
    all_gather x2 -> x0, blocking collectives: 166 us -> none  [the longest x1 83.5 us: on_device(): lax.all_gather(w_in_t, 'space', axis=0, tiled=True)]
    another operation x24 -> x0, loops' own time: 111 us -> none  [the longest x7 94.8 us: kernel_over_x(): return lax.map(kernel_over_y, jnp.arange(width, dtype=jnp.int32))]
    pallas_call x0 -> x1, Pallas kernels: none -> 69.9 us  [on_device(): pl.pallas_call(kernel_body, out_shape=(jax.ShapeDtypeStruct((CELLS, C), B...]
    add x98 -> x0, other arithmetic: 41.2 us -> none  [stencil_over_y(): inner = inner + window.astype(jnp.float32) * taps_y[along_z]]
    dynamic_slice x77 -> x0, local copies, waits for them, and re-layouts: 34.8 us -> none  [the longest x56 34.1 us: kernel_terms(): return lax.map(kernel_over_x, jnp.arange(width, dtype=jnp.int32))]
  transfers between devices with their start and end apart: 69 -> 0, of which waited for: 1 -> 0; matrix products, arithmetic and copies ran while one was open for 7% -> 0% of each run, Pallas kernels for 0% -> 0%
where the time goes in v1:
time: 82.9 us; the launch traced here: 82.5 us
  Pallas kernels  69.9 us (84%)
  local copies, waits for them, and re-layouts  10.4 us (13%)
  other arithmetic  1.5 us (2%)
    pallas_call x1, Pallas kernels, on_device(): pl.pallas_call(kernel_body, out_shape=(jax.ShapeDtypeStruct((CELLS, C), B...  69.9 us
    unnamed x29, local copies, waits for them, and re-layouts  8.51 us

profile of v1, /device:TPU:1, one launch (start us, length us, event | category | flops | bytes accessed | tf_op | source)
XLA Modules:
  0.0 82.5 jit_solution(3251423130466646879)
XLA Ops:
  0.6 0.0 copy-start.5
  0.7 0.8 copy.26
  1.4 0.8 fusion.7
  2.2 0.0 copy-start.10
  2.2 0.0 copy-start.11
  2.2 0.7 fusion.1.blk_ref
  3.0 0.0 copy-done.5
  3.0 0.0 copy-done.7
  3.0 0.0 copy-done.8
  3.0 0.0 copy-start
  3.0 1.0 %copy-done = f32[7,7,7,192]{3,2,1,0:T(8,128)S(1)} copy-done((f32[7,7,7,192]{3,2,1,0:T(8,128)S(1)}, f32[7,7,7,192]{3,2,1,0:T(8,128)}, u32[]{:S(2)}) %copy-start) | copy-done | bytes 263448
  4.0 0.9 %copy-done.1 = bf16[4,8,8,192]{3,2,1,0:T(8,128)(2,1)S(1)} copy-done((bf16[4,8,8,192]{3,2,1,0:T(8,128)(2,1)S(1)}, bf16[4,8,8,192]{3,2,1,0:T(8,128)(2,1)}, u32[]{:S(2)}) %copy-start.1) | copy-done | bytes 98328
  4.9 0.9 %copy-done.2 = bf16[4,8,8,192]{3,2,1,0:T(8,128)(2,1)S(1)} copy-done((bf16[4,8,8,192]{3,2,1,0:T(8,128)(2,1)S(1)}, bf16[4,8,8,192]{3,2,1,0:T(8,128)(2,1)}, u32[]{:S(2)}) %copy-start.2) | copy-done | bytes 98328
  5.8 0.8 %copy-done.3 = bf16[2,128,56]{2,1,0:T(8,128)(2,1)S(1)} copy-done((bf16[2,128,56]{2,1,0:T(8,128)(2,1)S(1)}, bf16[2,128,56]{2,1,0:T(8,128)(2,1)}, u32[]{:S(2)}) %copy-start.3) | copy-done | bytes 28696
  6.7 0.8 %copy-done.4 = bf16[256,64]{1,0:T(8,128)(2,1)S(1)} copy-done((bf16[256,64]{1,0:T(8,128)(2,1)S(1)}, bf16[256,64]{1,0:T(8,128)(2,1)}, u32[]{:S(2)}) %copy-start.4) | copy-done | bytes 32792
  7.5 0.7 copy-done.6
  8.2 69.9 %shard_map.230 = (bf16[256,192]{1,0:T(8,128)(2,1)S(1)}, bf16[256,192]{1,0:T(8,128)(2,1)S(1)}, f32[7,7,7,192]{3,2,1,0:T(8,128)S(1)}, f32[8,192]{1,0:T(8,128)S(1)}...) custom-call(bf16[256,192]{1,0:T(8,128)(2,1)S(1)} %bitcast.19, bf16[256,192]{1,0:T(8,128)(2,1)S(1)} %bitcast.20, ...), custom_call_target="tpu_custom_call" | custom-call | tf_op jit(solution)/shard_map/pallas_call | solution.py:460
  78.1 0.5 slice_bitcast_fusion
  78.6 0.6 fusion.8
  79.2 0.7 copy.32
  79.9 0.7 copy.33
  80.5 0.7 copy.34
  81.3 0.6 copy.35
  81.9 0.6 copy.36
  (11 shorter events, 0.0 us)
Async XLA Ops:
  0.6 2.3 %copy-start.5 = (bf16[2,64,128]{2,1,0:T(8,128)(2,1)S(1)}, bf16[2,64,128]{2,1,0:T(8,128)(2,1)}, u32[]{:S(2)}) copy-start(bf16[2,64,128]{2,1,0:T(8,128)(2,1)} %constant.13.clone.im_ref) | copy-start | bytes 98308
  2.2 0.8 copy-start.7
  2.2 0.8 copy-start.8
  2.2 0.8 copy-start.9
  2.2 0.8 copy-start.10
  2.2 0.8 copy-start.11
  3.0 1.0 %copy-start = (f32[7,7,7,192]{3,2,1,0:T(8,128)S(1)}, f32[7,7,7,192]{3,2,1,0:T(8,128)}, u32[]{:S(2)}) copy-start(f32[7,7,7,192]{3,2,1,0:T(8,128)} %ker_ref.1) | copy-start | bytes 790276
  4.0 0.9 %copy-start.1 = (bf16[4,8,8,192]{3,2,1,0:T(8,128)(2,1)S(1)}, bf16[4,8,8,192]{3,2,1,0:T(8,128)(2,1)}, u32[]{:S(2)}) copy-start(bf16[4,8,8,192]{3,2,1,0:T(8,128)(2,1)} %param.15) | copy-start | bytes 294916
  4.9 0.9 %copy-start.2 = (bf16[4,8,8,192]{3,2,1,0:T(8,128)(2,1)S(1)}, bf16[4,8,8,192]{3,2,1,0:T(8,128)(2,1)}, u32[]{:S(2)}) copy-start(bf16[4,8,8,192]{3,2,1,0:T(8,128)(2,1)} %param.16) | copy-start | bytes 294916
  5.8 0.8 %copy-start.3 = (bf16[2,128,56]{2,1,0:T(8,128)(2,1)S(1)}, bf16[2,128,56]{2,1,0:T(8,128)(2,1)}, u32[]{:S(2)}) copy-start(bf16[2,128,56]{2,1,0:T(8,128)(2,1)} %constant.12.clone.km_ref) | copy-start | bytes 86020
  6.7 0.8 %copy-start.4 = (bf16[256,64]{1,0:T(8,128)(2,1)S(1)}, bf16[256,64]{1,0:T(8,128)(2,1)}, u32[]{:S(2)}) copy-start(bf16[256,64]{1,0:T(8,128)(2,1)} %constant.11.clone.fm_ref) | copy-start | bytes 98308
  7.5 0.7 copy-start.6

commit v2 on v1

--- a/solution.py
+++ b/solution.py
@@ -22,7 +22,7 @@
 N = 11
 NF = 64
 UNITS = 6
-LANES = 512
+LANES = 384
 GROUPS = 7
 TILES = 2 * GROUPS
 
@@ -91,12 +91,15 @@
 
 
 def kernel_body(
-    x_ref, cot_ref, ker_ref, bdw_ref, gain_ref, bias_ref, blk_ref, bout_ref, gamma_ref,
-    fm_ref, km_ref, im_ref, lm_ref,
-    out_ref, dx_ref, dker_ref, vec_ref, dwi_ref, dwo_ref, dbi_ref,
+    x_hbm, cot_hbm, ker_hbm, bdw_hbm, gain_hbm, bias_hbm, win_hbm, bin_hbm, wout_hbm, bout_hbm,
+    gamma_hbm, fm_hbm, km_hbm, im_hbm, lm_hbm,
+    out_ref, dx_ref, dker_ref, vbdw_ref, vgain_ref, vbias_ref, dwi_ref, dbi_ref, dwo_ref,
+    vbout_ref, vgamma_ref,
+    x_ref, cot_ref, ker_ref, bdw_ref, gain_ref, bias_ref, win_ref, bin_ref, wout_ref, bout_ref,
+    gamma_ref, fm_ref, km_ref, im_ref, lm_ref, l_sem, blk_ref,
     halo_x, halo_d, wall, swall, r1, t1, t1b, r2, t2, t2b, r3,
     kpad, kf, xf, df, yf, gf, mixed, na, dba, branch, dnorm, dmb,
-    pay, payb, rx, zt, ztb, rz, agz, fin,
+    pay, payb, rx, zt, ztb, rz, agz, fin, wrk,
     s_halo, q_halo, s_ga, q_ga, s_gb, q_gb, s_gc, q_gc, s_hd, q_hd,
     s_rc, q_rc, s_rb, q_rb, s_ra, q_ra, s_px, q_px, s_pz, q_pz, s_az, q_az, s_ax, q_ax,
 ):
@@ -139,6 +142,16 @@
         for c in copies:
             c.wait_recv()
 
+    pairs = [
+        (win_hbm, win_ref), (bin_hbm, bin_ref), (wout_hbm, wout_ref), (ker_hbm, ker_ref),
+        (km_hbm, km_ref), (fm_hbm, fm_ref), (x_hbm, x_ref), (im_hbm, im_ref), (bdw_hbm, bdw_ref),
+        (gain_hbm, gain_ref), (bias_hbm, bias_ref), (cot_hbm, cot_ref), (gamma_hbm, gamma_ref),
+        (bout_hbm, bout_ref), (lm_hbm, lm_ref),
+    ]
+    loads = [pltpu.make_async_copy(a, b, l_sem.at[i]) for i, (a, b) in enumerate(pairs)]
+    for c in loads:
+        c.start()
+
     barrier = pltpu.get_barrier_semaphore()
     peers = [at_z(d) for d in range(1, NZ)] + [at_xc(k) for k in range(1, 2 * NX)] + [left, right]
     for dev in peers:
@@ -146,13 +159,25 @@
     pl.semaphore_wait(barrier, len(peers))
 
     halo = launch([
-        copy(x_ref.at[pl.ds(64, 192)], halo_x.at[0], s_halo.at[0], q_halo.at[0], right),
-        copy(x_ref.at[pl.ds(0, 192)], halo_x.at[1], s_halo.at[1], q_halo.at[1], left),
-    ])
+        copy(x_hbm.at[pl.ds(64, 192)], halo_x.at[0], s_halo.at[0], q_halo.at[0], right),
+        copy(x_hbm.at[pl.ds(0, 192)], halo_x.at[1], s_halo.at[1], q_halo.at[1], left),
+    ])
+    for c in loads[:3]:
+        c.wait()
+    row = lax.broadcasted_iota(jnp.int32, (8, 128), 0)
+    col = lax.broadcasted_iota(jnp.int32, (8, 128), 1)
+    wrk[...] = jnp.zeros_like(wrk)
+    wrk[0:UNITS, 0:C] = win_ref[...].astype(F32)
+    wrk[0:UNITS, 256:LANES] = wout_ref[:, 0:128].astype(F32)
+    wrk[0:UNITS, C:256] = wout_ref[:, 128:C].astype(F32)
+    wrk[UNITS : UNITS + 1, 0:UNITS] = bin_ref[...].astype(F32)
+    blk_ref[...] = wrk[...].astype(BF)
     gather_a = launch([
         copy(blk_ref, wall.at[0, 0, d], s_ga.at[d - 1], q_ga.at[d - 1], at_z(d)) for d in range(1, NZ)
     ])
     wall[0, 0, 0] = blk_ref[...]
+    for c in loads[3:]:
+        c.wait()
 
     kpad[...] = jnp.zeros_like(kpad)
     for a in range(W):
@@ -177,6 +202,11 @@
     gather_b = launch([
         copy(wall.at[0, 0], wall.at[0, d], s_gb.at[d - 1], q_gb.at[d - 1], at_x(d)) for d in range(1, NX)
     ])
+
+    def pass_on(d):
+        return launch([copy(wall.at[0, d], wall.at[1, d], s_gc.at[d], q_gc.at[d], partner)])
+
+    gather_c = {0: pass_on(0)}
 
     arrive(halo)
     has_left = (s > 0).astype(F32)
@@ -203,9 +233,6 @@
     for p in range(SX):
         mixed[64 * p : 64 * p + 64, :] = dot3(inv, yf[p]) + bdw_ref[...]
 
-    arrive(gather_b)
-    gather_c = launch([copy(wall.at[0], wall.at[1], s_gc.at[0], q_gc.at[0], partner)])
-
     mix = mixed[...]
     centred = mix - jnp.mean(mix, axis=-1, keepdims=True)
     inverse = lax.rsqrt(jnp.mean(centred * centred, axis=-1, keepdims=True) + 1e-06)
@@ -214,43 +241,62 @@
     lane = lax.broadcasted_iota(jnp.int32, (CELLS, 128), 1)
     na[:, 128:256] = jnp.where(lane == C - 128, 1.0, 0.0).astype(BF)
     na[:, 0:C] = (unit * gain_ref[...] + bias_ref[...]).astype(BF)
-    dba[:, 128:256] = jnp.zeros((CELLS, 128), BF)
-    dba[:, 0:C] = (gamma_ref[...] * cot_ref[...].astype(F32)).astype(BF)
+    d_branch = gamma_ref[...] * cot_ref[...].astype(F32)
+    dba[:, 0:128] = jnp.zeros((CELLS, 128), BF)
+    dba[:, 64:128] = d_branch[:, 128:C].astype(BF)
+    dba[:, 128:256] = d_branch[:, 0:128].astype(BF)
     branch[...] = jnp.zeros_like(branch)
     dnorm[...] = jnp.zeros_like(dnorm)
-
-    def units(dc):
-        def chunk(i, carry):
-            two = pl.ds(2 * i, 2)
-            rows = wall[dc, two].astype(F32).reshape(256, LANES).astype(BF)
-            win, wout = rows[:, 0:256], rows[:, 256:512]
-            normed, db = na[...], dba[...]
-            pre = dot_nt(normed, win)
-            half_erf = 0.5 * (1.0 + lax.erf(pre * root_half))
-            hidden = (pre * half_erf).astype(BF)
-            slope = half_erf + pre * jnp.exp(-0.5 * pre * pre) * inv_root_tau
-            branch[...] += dot(hidden, wout)
-            d_pre = (dot_nt(db, wout) * slope).astype(BF)
-            dnorm[...] += dot(d_pre, win)
-            dwi = (dot_tn(d_pre, normed) * scale).reshape(2, NZ, 8, 256)
-            dwo = (dot_tn(hidden, db) * scale).reshape(2, NZ, 8, 256)
+    lane8 = lax.broadcasted_iota(jnp.int32, (2 * NZ, 8, 128), 2)
+    row8 = lax.broadcasted_iota(jnp.int32, (2 * NZ, 8, 128), 1)
+
+    def units(dc, i):
+        two = pl.ds(2 * i, 2)
+        block = wall[dc, two].astype(F32).reshape(2 * NZ, 8, LANES)
+        t_a, t_b = block[:, :, 0:128], block[:, :, 128:256]
+        tail = jnp.broadcast_to(t_a[:, UNITS : UNITS + 1, :], t_a.shape)
+        b_col = jnp.sum(jnp.where(row8 == lane8, tail, 0.0), axis=2, keepdims=True)
+        t_bias = jnp.where(lane8 == C - 128, b_col, t_b)
+        win = jnp.concatenate([t_a.reshape(256, 128), t_bias.reshape(256, 128)], axis=1).astype(BF)
+        wout = block[:, :, 128:LANES].reshape(256, 256).astype(BF)
+        normed, db = na[...], dba[...]
+        pre = dot_nt(normed, win)
+        half_erf = 0.5 * (1.0 + lax.erf(pre * root_half))
+        hidden = (pre * half_erf).astype(BF)
+        slope = half_erf + pre * jnp.exp(-0.5 * pre * pre) * inv_root_tau
+        branch[...] += dot(hidden, wout)
+        d_pre = (dot_nt(db, wout) * slope).astype(BF)
+        dnorm[...] += dot(d_pre, win)
+        dwi = (dot_tn(d_pre, normed) * scale).reshape(2 * NZ, 8, 256)
+        dwo = (dot_tn(hidden, db) * scale).reshape(2 * NZ, 8, 256)
+        g_a, g_b = dwi[:, :, 0:128], dwi[:, :, 128:256]
+        g_col = jnp.broadcast_to(g_b[:, :, C - 128 : C - 127], g_b.shape)
+        g_row = jnp.sum(jnp.where(row8 == lane8, g_col, 0.0), axis=1, keepdims=True)
+        g_a = jnp.where(row8 == UNITS, jnp.broadcast_to(g_row, g_a.shape), g_a)
+        g_b = jnp.where(lane8 < C - 128, g_b, dwo[:, :, 0:128])
+        parts = (g_a, g_b, dwo[:, :, 128:256])
+        for j, part in enumerate(parts):
+            part = part.reshape(2, NZ, 8, 128)
             if dc == 0:
-                t1[two, :, :, 0:256] = dwi
-                t1[two, :, :, 256:512] = dwo
+                t1[two, :, :, 128 * j : 128 * j + 128] = part
             else:
-                swall[two, :, :, 0:256] = dwi.astype(BF)
-                swall[two, :, :, 256:512] = dwo.astype(BF)
-            return carry
-
-        lax.fori_loop(0, 2, chunk, 0)
-
-    units(0)
-    arrive(gather_c)
-    units(1)
-    scatter_c = launch([copy(swall, r1, s_rc.at[0], q_rc.at[0], partner)])
+                swall[two, :, :, 128 * j : 128 * j + 128] = part.astype(BF)
+
+    for d in (1, 3, 2):
+        arrive([gather_b[d - 1]])
+        gather_c[d] = pass_on(d)
+        if d == 1:
+            units(0, 0)
+    units(0, 1)
+    scatter_c = []
+    for i in range(2):
+        arrive(gather_c[2 * i] + gather_c[2 * i + 1])
+        units(1, i)
+        two = pl.ds(2 * i, 2)
+        scatter_c += launch([copy(swall.at[two], r1.at[two], s_rc.at[i], q_rc.at[i], partner)])
 
     cot = cot_ref[...].astype(F32)
-    full = branch[:, 0:C] + bout_ref[...]
+    full = jnp.concatenate([branch[:, 128:256], branch[:, 64:128]], axis=1) + bout_ref[...]
     out_ref[...] = (x_ref[...].astype(F32) + gamma_ref[...] * full).astype(BF)
     v_gamma = jnp.sum(cot * full, axis=0, keepdims=True)
     v_bout = jnp.sum(gamma_ref[...] * cot, axis=0, keepdims=True)
@@ -389,11 +435,9 @@
     for d in range(NZ - 1):
         mine = mine + r3[d].astype(F32)
     dwi_ref[...] = mine[0:UNITS, 0:C]
-    dwo_ref[...] = mine[0:UNITS, 256 : 256 + C]
-    row = lax.broadcasted_iota(jnp.int32, (8, 128), 0)
-    col = lax.broadcasted_iota(jnp.int32, (8, 128), 1)
-    bias_col = jnp.broadcast_to(mine[:, C : C + 1], (8, 128))
-    dbi_ref[...] = jnp.sum(jnp.where(row == col, bias_col, 0.0), axis=0, keepdims=True)
+    dwo_ref[:, 0:128] = mine[0:UNITS, 256:LANES]
+    dwo_ref[:, 128:C] = mine[0:UNITS, C:256]
+    dbi_ref[...] = mine[UNITS : UNITS + 1, 0:UNITS]
 
     arrive(gather_x)
     for group in range(W * W):
@@ -402,29 +446,40 @@
         dker_ref[group // W, group % W, :, 0:128] = first[0:W]
         dker_ref[group // W, group % W, :, 128:C] = second[0:W, 0 : C - 128]
         if group < 5:
-            vec_ref[group : group + 1, 0:128] = first[W : W + 1]
-            vec_ref[group : group + 1, 128:C] = second[W : W + 1, 0 : C - 128]
+            v_ref = (vbdw_ref, vgain_ref, vbias_ref, vbout_ref, vgamma_ref)[group]
+            v_ref[:, 0:128] = first[W : W + 1]
+            v_ref[:, 128:C] = second[W : W + 1, 0 : C - 128]
 
     for c in pending:
         c.wait_send()
+
+
+def emit_body(*refs):
+    n = (len(refs) - 1) // 2
+    sems = refs[-1]
+    copies = [pltpu.make_async_copy(refs[i], refs[n + i], sems.at[i]) for i in range(n)]
+    for c in copies:
+        c.start()
+    for c in copies:
+        c.wait()
 
 
 def on_device(
     features, cotangent, kernel, b_dw, ln_gain, ln_bias, w_in_t, b_in, w_out, b_out, gamma
 ):
-    block = jnp.concatenate(
-        [
-            jnp.pad(jnp.concatenate([w_in_t, b_in[:, None]], axis=1), ((0, 2), (0, 255 - C))),
-            jnp.pad(w_out, ((0, 2), (0, 256 - C))),
-        ],
-        axis=1,
-    )
-    fm, km, im, lm = (jnp.asarray(m) for m in transforms())
+    operands = [
+        features.reshape(CELLS, C), cotangent.reshape(CELLS, C), kernel,
+        b_dw.reshape(1, C), ln_gain.reshape(1, C), ln_bias.reshape(1, C), w_in_t,
+        b_in.reshape(1, UNITS), w_out, b_out.reshape(1, C), gamma.reshape(1, C),
+    ] + [jnp.asarray(m) for m in transforms()]
     vm = pl.BlockSpec(memory_space=pltpu.VMEM)
+    hbm = pl.BlockSpec(memory_space=pltpu.HBM)
     dma = pltpu.SemaphoreType.DMA
-    counts = [2, NZ - 1, NX - 1, 1, 2, 1, NX - 1, NZ - 1, 2 * NX - 1, NZ - 1, NZ - 1, 2 * NX - 1]
+    counts = [2, NZ - 1, NX - 1, NX, 2, 2, NX - 1, NZ - 1, 2 * NX - 1, NZ - 1, NZ - 1, 2 * NX - 1]
     sems = [dma((n,)) for n in counts for _ in range(2)]
-    scratch = [
+    scratch = [pltpu.VMEM(o.shape, o.dtype) for o in operands] + [
+        dma((len(operands),)),
+        pltpu.VMEM((8, LANES), BF),
         pltpu.VMEM((2, 192, C), BF),
         pltpu.VMEM((2, 192, C), BF),
         pltpu.VMEM((2, NX, NZ, 8, LANES), BF),
@@ -456,33 +511,41 @@
         pltpu.VMEM((NZ - 1, 8, 128), BF),
         pltpu.VMEM((NZ, 8, 128), BF),
         pltpu.VMEM((2 * NX, NZ, 8, 128), BF),
+        pltpu.VMEM((8, LANES), F32),
     ]
-    out, dx, dker, vec, dwi, dwo, dbi = pl.pallas_call(
+    vec = jax.ShapeDtypeStruct((1, C), F32)
+    shapes = (
+        jax.ShapeDtypeStruct((CELLS, C), BF),
+        jax.ShapeDtypeStruct((CELLS, C), BF),
+        jax.ShapeDtypeStruct((W, W, W, C), F32),
+        vec, vec, vec,
+        jax.ShapeDtypeStruct((UNITS, C), F32),
+        jax.ShapeDtypeStruct((1, UNITS), F32),
+        jax.ShapeDtypeStruct((UNITS, C), F32),
+        vec, vec,
+    )
+    results = pl.pallas_call(
         kernel_body,
-        out_shape=(
-            jax.ShapeDtypeStruct((CELLS, C), BF),
-            jax.ShapeDtypeStruct((CELLS, C), BF),
-            jax.ShapeDtypeStruct((W, W, W, C), F32),
-            jax.ShapeDtypeStruct((8, C), F32),
-            jax.ShapeDtypeStruct((UNITS, C), F32),
-            jax.ShapeDtypeStruct((UNITS, C), F32),
-            jax.ShapeDtypeStruct((1, 128), F32),
-        ),
-        in_specs=[vm] * 13,
-        out_specs=(vm,) * 7,
+        out_shape=shapes,
+        in_specs=[hbm] * len(operands),
+        out_specs=(vm,) * len(shapes),
         scratch_shapes=scratch + sems,
         compiler_params=pltpu.CompilerParams(
             collective_id=0, has_side_effects=True, vmem_limit_bytes=48 * 1024 * 1024
         ),
-    )(
-        features.reshape(CELLS, C), cotangent.reshape(CELLS, C), kernel,
-        b_dw.reshape(1, C), ln_gain.reshape(1, C), ln_bias.reshape(1, C), block,
-        b_out.reshape(1, C), gamma.reshape(1, C), fm, km, im, lm,
-    )
-    shape = features.shape
+    )(*[pltpu.with_memory_space_constraint(o, pltpu.HBM) for o in operands])
+    results = pl.pallas_call(
+        emit_body,
+        out_shape=shapes,
+        in_specs=[vm] * len(shapes),
+        out_specs=(hbm,) * len(shapes),
+        scratch_shapes=[dma((len(shapes),))],
+    )(*[pltpu.with_memory_space_constraint(o, pltpu.VMEM) for o in results])
+    out, dx, dker, bdw, gain, bias, dwi, dbi, dwo, bout, gam = results
     return (
-        out.reshape(shape), dx.reshape(shape), dker,
-        vec[0], vec[1], vec[2], dwi, dbi[0, 0:UNITS], dwo, vec[3], vec[4],
+        out.reshape(features.shape), dx.reshape(features.shape), dker,
+        bdw.reshape(C), gain.reshape(C), bias.reshape(C), dwi, dbi.reshape(UNITS), dwo,
+        bout.reshape(C), gam.reshape(C),
     )
 
 

time: 82.9 us -> 65.8 us (0.79)
  local copies, waits for them, and re-layouts: 10.4 us -> 0 us
  Pallas kernels: 69.9 us -> 65 us
  other arithmetic: 1.5 us -> 0 us
    unnamed x29 -> x0, local copies, waits for them, and re-layouts: 8.51 us -> none
    pallas_call x1 -> x2, Pallas kernels: 69.9 us -> 65 us  [the longest x1 64.1 us: on_device(): pl.pallas_call(kernel_body, out_shape=shapes, in_specs=[hbm] * len(operan...]
    concatenate x2 -> x0, other arithmetic: 1.5 us -> none  [the longest x1 0.76 us: on_device(): jnp.concatenate([w_in_t, b_in[:, None]], axis=1)]
where the time goes in v2:
time: 65.8 us; the launch traced here: 65.7 us
  Pallas kernels  65 us (99%)
  between operations  0.66 us (1%)
    pallas_call x1, Pallas kernels, on_device(): pl.pallas_call(kernel_body, out_shape=shapes, in_specs=[hbm] * len(operan...  64.1 us

profile of v2, /device:TPU:1, one launch (start us, length us, event | category | flops | bytes accessed | tf_op | source)
XLA Modules:
  0.0 65.7 jit_solution(1740075140103598699)
XLA Ops:
  0.6 64.1 %shard_map.230 = (bf16[256,192]{1,0:T(8,128)(2,1)S(1)}, bf16[256,192]{1,0:T(8,128)(2,1)S(1)}, f32[7,7,7,192]{3,2,1,0:T(8,128)S(1)}, f32[1,192]{1,0:T(1,128)S(1)}...) custom-call(bf16[256,192]{1,0:T(8,128)(2,1)} %bitcast.16, ...), custom_call_target="tpu_custom_call" | custom-call | tf_op jit(solution)/shard_map/pallas_call | solution.py:527
  64.7 1.0 %shard_map.231 = (bf16[256,192]{1,0:T(8,128)(2,1)}, bf16[256,192]{1,0:T(8,128)(2,1)}, f32[7,7,7,192]{3,2,1,0:T(8,128)}, f32[1,192]{1,0:T(1,128)}, f32[1,192]{1,0...) custom-call(bf16[256,192]{1,0:T(8,128)(2,1)S(1)} %get-tuple-element., ...), custom_call_target="tpu_custom_call" | custom-call | tf_op jit(solution)/shard_map/pallas_call | solution.py:537

commit v3 on v2

--- a/solution.py
+++ b/solution.py
@@ -23,8 +23,9 @@
 NF = 64
 UNITS = 6
 LANES = 384
-GROUPS = 7
-TILES = 2 * GROUPS
+CHUNK = 10
+ORDER = (0, 1, 15, 2, 14, 3, 13, 4, 12, 5, 11, 6, 10, 7, 9, 8)
+BANDS = ((0, 6), (6, 11), (11, 16))
 
 
 def split_np(m):
@@ -99,7 +100,7 @@
     gamma_ref, fm_ref, km_ref, im_ref, lm_ref, l_sem, blk_ref,
     halo_x, halo_d, wall, swall, r1, t1, t1b, r2, t2, t2b, r3,
     kpad, kf, xf, df, yf, gf, mixed, na, dba, branch, dnorm, dmb,
-    pay, payb, rx, zt, ztb, rz, agz, fin, wrk,
+    pay, payb, rx, zt, ztb, rz, agz, fin, wrk, hid, dpb,
     s_halo, q_halo, s_ga, q_ga, s_gb, q_gb, s_gc, q_gc, s_hd, q_hd,
     s_rc, q_rc, s_rb, q_rb, s_ra, q_ra, s_px, q_px, s_pz, q_pz, s_az, q_az, s_ax, q_ax,
 ):
@@ -158,10 +159,6 @@
         pl.semaphore_signal(barrier, inc=1, device_id=dev, device_id_type=MESH)
     pl.semaphore_wait(barrier, len(peers))
 
-    halo = launch([
-        copy(x_hbm.at[pl.ds(64, 192)], halo_x.at[0], s_halo.at[0], q_halo.at[0], right),
-        copy(x_hbm.at[pl.ds(0, 192)], halo_x.at[1], s_halo.at[1], q_halo.at[1], left),
-    ])
     for c in loads[:3]:
         c.wait()
     row = lax.broadcasted_iota(jnp.int32, (8, 128), 0)
@@ -173,7 +170,12 @@
     wrk[UNITS : UNITS + 1, 0:UNITS] = bin_ref[...].astype(F32)
     blk_ref[...] = wrk[...].astype(BF)
     gather_a = launch([
-        copy(blk_ref, wall.at[0, 0, d], s_ga.at[d - 1], q_ga.at[d - 1], at_z(d)) for d in range(1, NZ)
+        copy(blk_ref, wall.at[0, 0, i], s_ga.at[i - 1], q_ga.at[i - 1], at_z(ORDER[i]))
+        for i in range(NZ - 1, 0, -1)
+    ])[::-1]
+    halo = launch([
+        copy(x_hbm.at[pl.ds(64, 192)], halo_x.at[0], s_halo.at[0], q_halo.at[0], right),
+        copy(x_hbm.at[pl.ds(0, 192)], halo_x.at[1], s_halo.at[1], q_halo.at[1], left),
     ])
     wall[0, 0, 0] = blk_ref[...]
     for c in loads[3:]:
@@ -197,16 +199,6 @@
     lax.fori_loop(0, W, ker_step, 0)
     for p in range(SX):
         xf[3 + p] = transform(x_ref[64 * p : 64 * p + 64, :])
-
-    arrive(gather_a)
-    gather_b = launch([
-        copy(wall.at[0, 0], wall.at[0, d], s_gb.at[d - 1], q_gb.at[d - 1], at_x(d)) for d in range(1, NX)
-    ])
-
-    def pass_on(d):
-        return launch([copy(wall.at[0, d], wall.at[1, d], s_gc.at[d], q_gc.at[d], partner)])
-
-    gather_c = {0: pass_on(0)}
 
     arrive(halo)
     has_left = (s > 0).astype(F32)
@@ -250,6 +242,28 @@
     lane8 = lax.broadcasted_iota(jnp.int32, (2 * NZ, 8, 128), 2)
     row8 = lax.broadcasted_iota(jnp.int32, (2 * NZ, 8, 128), 1)
 
+    gather_b, gather_c = {}, {}
+
+    def band(dc, d, k):
+        lo, hi = BANDS[k]
+        return wall.at[dc, d, pl.ds(lo, hi - lo)]
+
+    def pass_on(d, k):
+        i = 3 * d + k
+        gather_c[d, k] = launch([
+            copy(band(0, d, k), band(1, d, k), s_gc.at[i], q_gc.at[i], partner)
+        ])
+
+    for k in range(3):
+        lo, hi = BANDS[k]
+        arrive(gather_a[max(lo, 1) - 1 : hi - 1])
+        for d in (2, 1, 3):
+            i = 3 * (d - 1) + k
+            gather_b[d, k] = launch([
+                copy(band(0, 0, k), band(0, d, k), s_gb.at[i], q_gb.at[i], at_x(d))
+            ])
+        pass_on(0, k)
+
     def units(dc, i):
         two = pl.ds(2 * i, 2)
         block = wall[dc, two].astype(F32).reshape(2 * NZ, 8, LANES)
@@ -263,10 +277,16 @@
         pre = dot_nt(normed, win)
         half_erf = 0.5 * (1.0 + lax.erf(pre * root_half))
         hidden = (pre * half_erf).astype(BF)
+        hid[dc, i] = hidden
         slope = half_erf + pre * jnp.exp(-0.5 * pre * pre) * inv_root_tau
         branch[...] += dot(hidden, wout)
         d_pre = (dot_nt(db, wout) * slope).astype(BF)
+        dpb[dc, i] = d_pre
         dnorm[...] += dot(d_pre, win)
+
+    def gradients(dc, i):
+        two = pl.ds(2 * i, 2)
+        hidden, d_pre, normed, db = hid[dc, i], dpb[dc, i], na[...], dba[...]
         dwi = (dot_tn(d_pre, normed) * scale).reshape(2 * NZ, 8, 256)
         dwo = (dot_tn(hidden, db) * scale).reshape(2 * NZ, 8, 256)
         g_a, g_b = dwi[:, :, 0:128], dwi[:, :, 128:256]
@@ -282,22 +302,20 @@
             else:
                 swall[two, :, :, 128 * j : 128 * j + 128] = part.astype(BF)
 
-    for d in (1, 3, 2):
-        arrive([gather_b[d - 1]])
-        gather_c[d] = pass_on(d)
-        if d == 1:
-            units(0, 0)
-    units(0, 1)
-    scatter_c = []
+    for k in range(3):
+        for d in (1, 3, 2):
+            arrive(gather_b[d, k])
+            pass_on(d, k)
     for i in range(2):
-        arrive(gather_c[2 * i] + gather_c[2 * i + 1])
+        units(0, i)
+    for i in range(2):
+        for d in (2 * i, 2 * i + 1):
+            for k in range(3):
+                arrive(gather_c[d, k])
         units(1, i)
-        two = pl.ds(2 * i, 2)
-        scatter_c += launch([copy(swall.at[two], r1.at[two], s_rc.at[i], q_rc.at[i], partner)])
 
     cot = cot_ref[...].astype(F32)
     full = jnp.concatenate([branch[:, 128:256], branch[:, 64:128]], axis=1) + bout_ref[...]
-    out_ref[...] = (x_ref[...].astype(F32) + gamma_ref[...] * full).astype(BF)
     v_gamma = jnp.sum(cot * full, axis=0, keepdims=True)
     v_bout = jnp.sum(gamma_ref[...] * cot, axis=0, keepdims=True)
 
@@ -338,13 +356,16 @@
         for b in range(W):
             group = a * W + b
             block = taps[8 * b : 8 * b + 8, :]
-            q, t = group // GROUPS, 2 * (group % GROUPS)
+            q, t, r, u, at = spot(group)
             pay[q, t] = block[:, 0:128]
-            pay[q, t + 1, :, 0 : C - 128] = block[:, 128:C]
+            pay[r, u, :, at : at + C - 128] = block[:, 128:C]
     for i, v in enumerate(vectors):
-        pay[0, 2 * i, W : W + 1, :] = v[:, 0:128] * scale
-        pay[0, 2 * i + 1, W : W + 1, 0 : C - 128] = v[:, 128:C] * scale
+        q, t, r, u, at = spot(i)
+        pay[q, t, W : W + 1, :] = v[:, 0:128] * scale
+        pay[r, u, W : W + 1, at : at + C - 128] = v[:, 128:C] * scale
     payb[...] = pay[...].astype(BF)
+    zt[pl.ds(CHUNK, NZ - CHUNK)] = jnp.zeros((NZ - CHUNK, 8, 128), F32)
+    ztb[pl.ds(CHUNK, NZ - CHUNK)] = jnp.zeros((NZ - CHUNK, 8, 128), BF)
 
     def chunk_of(k):
         px = lax.rem(x + k % NX, NX)
@@ -357,6 +378,17 @@
         for k in range(1, 2 * NX)
     ])
 
+    scatter_c = []
+    for i in range(2):
+        gradients(1, i)
+        two = pl.ds(2 * i, 2)
+        scatter_c += launch([copy(swall.at[two], r1.at[two], s_rc.at[i], q_rc.at[i], partner)])
+    arrive(halo2)
+    for p in range(3):
+        df[p] = transform(halo_d[0, 64 * p : 64 * p + 64, :]) * has_left
+        df[7 + p] = transform(halo_d[1, 64 * p : 64 * p + 64, :]) * has_right
+    for i in range(2):
+        gradients(0, i)
     arrive(scatter_c)
 
     def add_core(i, carry):
@@ -370,20 +402,18 @@
         copy(t1b.at[d], r2.at[d - 1], s_rb.at[d - 1], q_rb.at[d - 1], at_x(-d)) for d in range(1, NX)
     ])
 
-    arrive(halo2)
-    for p in range(3):
-        df[p] = transform(halo_d[0, 64 * p : 64 * p + 64, :]) * has_left
-        df[7 + p] = transform(halo_d[1, 64 * p : 64 * p + 64, :]) * has_right
-
     arrive(sum_x)
     total = pay[own]
     for k in range(2 * NX - 1):
         total = total + rx[k].astype(F32)
-    zt[...] = total
-    ztb[...] = total.astype(BF)
+    zt[pl.ds(0, CHUNK)] = total
+    ztb[pl.ds(0, CHUNK)] = total.astype(BF)
     sum_z = launch([
-        copy(ztb.at[lax.rem(z + d, NZ)], rz.at[d - 1], s_pz.at[d - 1], q_pz.at[d - 1], at_z(d))
-        for d in range(1, NZ)
+        copy(
+            ztb.at[lax.rem(z + ORDER[i], NZ)], rz.at[i - 1], s_pz.at[i - 1], q_pz.at[i - 1],
+            at_z(ORDER[i]),
+        )
+        for i in range(NZ - 1, 0, -1)
     ])
 
     def back_step(g, carry):
@@ -408,26 +438,30 @@
     t2[...] = t2v
     t2b[...] = t2v.astype(BF)
     scatter_a = launch([
-        copy(t2b.at[d], r3.at[d - 1], s_ra.at[d - 1], q_ra.at[d - 1], at_z(-d)) for d in range(1, NZ)
+        copy(t2b.at[i], r3.at[i - 1], s_ra.at[i - 1], q_ra.at[i - 1], at_z(-ORDER[i]))
+        for i in range(NZ - 1, 0, -1)
     ])
 
     arrive(sum_z)
     tile = zt[z]
-    for d in range(NZ - 1):
-        tile = tile + rz[d].astype(F32)
+    for i in range(NZ - 1):
+        tile = tile + rz[i].astype(F32)
     agz[z] = tile.astype(BF)
     gather_z = launch([
-        copy(agz.at[z], agz.at[z], s_az.at[d - 1], q_az.at[d - 1], at_z(d)) for d in range(1, NZ)
-    ])
-
+        copy(agz.at[z], agz.at[z], s_az.at[i - 1], q_az.at[i - 1], at_z(ORDER[i]))
+        for i in range(NZ - 1, 0, -1)
+    ])
+
+    full = jnp.concatenate([branch[:, 128:256], branch[:, 64:128]], axis=1) + bout_ref[...]
+    out_ref[...] = (x_ref[...].astype(F32) + gamma_ref[...] * full).astype(BF)
     for p in range(SX):
         rows = slice(64 * p, 64 * p + 64)
         dx_ref[rows, :] = (cot_ref[rows, :].astype(F32) + dot3(inv, yf[p])).astype(BF)
 
     arrive(gather_z)
-    fin[own] = agz[...]
+    fin[own] = agz[pl.ds(0, CHUNK)]
     gather_x = launch([
-        copy(agz, fin.at[own], s_ax.at[k - 1], q_ax.at[k - 1], at_xc(k)) for k in range(1, 2 * NX)
+        copy(agz.at[pl.ds(0, CHUNK)], fin.at[own], s_ax.at[k - 1], q_ax.at[k - 1], at_xc(k)) for k in range(1, 2 * NX)
     ])
 
     arrive(scatter_a)
@@ -441,17 +475,23 @@
 
     arrive(gather_x)
     for group in range(W * W):
-        q, t = group // GROUPS, 2 * (group % GROUPS)
-        first, second = fin[q, t].astype(F32), fin[q, t + 1].astype(F32)
+        q, t, r, u, at = spot(group)
+        first, second = fin[q, t].astype(F32), fin[r, u].astype(F32)[:, at : at + C - 128]
         dker_ref[group // W, group % W, :, 0:128] = first[0:W]
-        dker_ref[group // W, group % W, :, 128:C] = second[0:W, 0 : C - 128]
+        dker_ref[group // W, group % W, :, 128:C] = second[0:W]
         if group < 5:
             v_ref = (vbdw_ref, vgain_ref, vbias_ref, vbout_ref, vgamma_ref)[group]
             v_ref[:, 0:128] = first[W : W + 1]
-            v_ref[:, 128:C] = second[W : W + 1, 0 : C - 128]
+            v_ref[:, 128:C] = second[W : W + 1]
 
     for c in pending:
         c.wait_send()
+
+
+def spot(group):
+    first = 3 * (group // 2)
+    whole, part = first + group % 2, first + 2
+    return whole // CHUNK, whole % CHUNK, part // CHUNK, part % CHUNK, (C - 128) * (group % 2)
 
 
 def emit_body(*refs):
@@ -475,7 +515,7 @@
     vm = pl.BlockSpec(memory_space=pltpu.VMEM)
     hbm = pl.BlockSpec(memory_space=pltpu.HBM)
     dma = pltpu.SemaphoreType.DMA
-    counts = [2, NZ - 1, NX - 1, NX, 2, 2, NX - 1, NZ - 1, 2 * NX - 1, NZ - 1, NZ - 1, 2 * NX - 1]
+    counts = [2, NZ - 1, 9, 12, 2, 2, NX - 1, NZ - 1, 2 * NX - 1, NZ - 1, NZ - 1, 2 * NX - 1]
     sems = [dma((n,)) for n in counts for _ in range(2)]
     scratch = [pltpu.VMEM(o.shape, o.dtype) for o in operands] + [
         dma((len(operands),)),
@@ -503,15 +543,17 @@
         pltpu.VMEM((CELLS, 256), F32),
         pltpu.VMEM((CELLS, 256), F32),
         pltpu.VMEM((CELLS, C), BF),
-        pltpu.VMEM((2 * NX, NZ, 8, 128), F32),
-        pltpu.VMEM((2 * NX, NZ, 8, 128), BF),
-        pltpu.VMEM((2 * NX - 1, NZ, 8, 128), BF),
+        pltpu.VMEM((2 * NX, CHUNK, 8, 128), F32),
+        pltpu.VMEM((2 * NX, CHUNK, 8, 128), BF),
+        pltpu.VMEM((2 * NX - 1, CHUNK, 8, 128), BF),
         pltpu.VMEM((NZ, 8, 128), F32),
         pltpu.VMEM((NZ, 8, 128), BF),
         pltpu.VMEM((NZ - 1, 8, 128), BF),
         pltpu.VMEM((NZ, 8, 128), BF),
-        pltpu.VMEM((2 * NX, NZ, 8, 128), BF),
+        pltpu.VMEM((2 * NX, CHUNK, 8, 128), BF),
         pltpu.VMEM((8, LANES), F32),
+        pltpu.VMEM((2, 2, CELLS, 256), BF),
+        pltpu.VMEM((2, 2, CELLS, 256), BF),
     ]
     vec = jax.ShapeDtypeStruct((1, C), F32)
     shapes = (

time: 65.8 us -> 61.5 us (0.935)
  Pallas kernels: 65 us -> 60.8 us
    pallas_call x1, Pallas kernels: 64.1 us -> 59.8 us  [on_device(): pl.pallas_call(kernel_body, out_shape=shapes, in_specs=[hbm] * len(operan...]
where the time goes in v3:
time: 61.5 us; the launch traced here: 61.4 us
  Pallas kernels  60.8 us (99%)
  between operations  0.66 us (1%)
    pallas_call x1, Pallas kernels, on_device(): pl.pallas_call(kernel_body, out_shape=shapes, in_specs=[hbm] * len(operan...  59.8 us

profile of v3, /device:TPU:1, one launch (start us, length us, event | category | flops | bytes accessed | tf_op | source)
XLA Modules:
  0.0 61.4 jit_solution(12619935150036997016)
XLA Ops:
  0.6 59.8 %shard_map.230 = (bf16[256,192]{1,0:T(8,128)(2,1)S(1)}, bf16[256,192]{1,0:T(8,128)(2,1)S(1)}, f32[7,7,7,192]{3,2,1,0:T(8,128)S(1)}, f32[1,192]{1,0:T(1,128)S(1)}...) custom-call(bf16[256,192]{1,0:T(8,128)(2,1)} %bitcast.16, ...), custom_call_target="tpu_custom_call" | custom-call | tf_op jit(solution)/shard_map/pallas_call | solution.py:569
  60.5 1.0 %shard_map.231 = (bf16[256,192]{1,0:T(8,128)(2,1)}, bf16[256,192]{1,0:T(8,128)(2,1)}, f32[7,7,7,192]{3,2,1,0:T(8,128)}, f32[1,192]{1,0:T(1,128)}, f32[1,192]{1,0...) custom-call(bf16[256,192]{1,0:T(8,128)(2,1)S(1)} %get-tuple-element., ...), custom_call_target="tpu_custom_call" | custom-call | tf_op jit(solution)/shard_map/pallas_call | solution.py:579

commit v4 on v3

--- a/solution.py
+++ b/solution.py
@@ -25,7 +25,8 @@
 LANES = 384
 CHUNK = 10
 ORDER = (0, 1, 15, 2, 14, 3, 13, 4, 12, 5, 11, 6, 10, 7, 9, 8)
-BANDS = ((0, 6), (6, 11), (11, 16))
+BANDS = ((0, 8), (8, 12), (12, 16))
+HALF = NZ // 2
 
 
 def split_np(m):
@@ -65,8 +66,7 @@
     inv = (fwd * scale).T
     ker = table(tap // 8 - 3, tap % 8 - 3, live, 1.0)
     lag = (table(tap // 8 - 3, tap % 8 - 3, live, -1.0) * scale).T
-    fm = np.concatenate(split_np(fwd), axis=0)
-    return fm, np.stack(split_np(ker)), np.stack(split_np(inv)), np.stack(split_np(lag))
+    return tuple(np.concatenate(split_np(m), axis=0) for m in (fwd, ker, inv, lag))
 
 
 def dot(a, b):
@@ -88,7 +88,9 @@
 
 def dot3(m, value):
     high, low = halves(value)
-    return dot(m[0], high) + dot(m[1], high) + dot(m[0], low)
+    rows = m.shape[0] // 2
+    both = dot(m, high)
+    return both[:rows] + both[rows:] + dot(m[:rows], low)
 
 
 def kernel_body(
@@ -139,10 +141,19 @@
         pending.extend(copies)
         return copies
 
+    def flush():
+        for c in pending:
+            c.wait_send()
+        pending.clear()
+
     def arrive(copies):
         for c in copies:
             c.wait_recv()
 
+    barrier = pltpu.get_barrier_semaphore()
+    peers = [at_z(d) for d in ORDER[:0:-1]] + [at_xc(k) for k in range(1, 2 * NX)] + [left, right]
+    for dev in peers:
+        pl.semaphore_signal(barrier, inc=1, device_id=dev, device_id_type=MESH)
     pairs = [
         (win_hbm, win_ref), (bin_hbm, bin_ref), (wout_hbm, wout_ref), (ker_hbm, ker_ref),
         (km_hbm, km_ref), (fm_hbm, fm_ref), (x_hbm, x_ref), (im_hbm, im_ref), (bdw_hbm, bdw_ref),
@@ -152,12 +163,6 @@
     loads = [pltpu.make_async_copy(a, b, l_sem.at[i]) for i, (a, b) in enumerate(pairs)]
     for c in loads:
         c.start()
-
-    barrier = pltpu.get_barrier_semaphore()
-    peers = [at_z(d) for d in range(1, NZ)] + [at_xc(k) for k in range(1, 2 * NX)] + [left, right]
-    for dev in peers:
-        pl.semaphore_signal(barrier, inc=1, device_id=dev, device_id_type=MESH)
-    pl.semaphore_wait(barrier, len(peers))
 
     for c in loads[:3]:
         c.wait()
@@ -169,6 +174,8 @@
     wrk[0:UNITS, C:256] = wout_ref[:, 128:C].astype(F32)
     wrk[UNITS : UNITS + 1, 0:UNITS] = bin_ref[...].astype(F32)
     blk_ref[...] = wrk[...].astype(BF)
+    pl.semaphore_wait(barrier, len(peers))
+
     gather_a = launch([
         copy(blk_ref, wall.at[0, 0, i], s_ga.at[i - 1], q_ga.at[i - 1], at_z(ORDER[i]))
         for i in range(NZ - 1, 0, -1)
@@ -190,7 +197,7 @@
         both = dot(fm_ref[...], rows)
         return both[: 2 * NF] + both[2 * NF :]
 
-    km = (km_ref[0], km_ref[1])
+    km = km_ref[...]
 
     def ker_step(a, carry):
         kf[a] = dot3(km, kpad[a])
@@ -221,7 +228,7 @@
         return carry
 
     lax.fori_loop(0, NF // 8, forward_step, 0)
-    inv = (im_ref[0], im_ref[1])
+    inv = im_ref[...]
     for p in range(SX):
         mixed[64 * p : 64 * p + 64, :] = dot3(inv, yf[p]) + bdw_ref[...]
 
@@ -239,6 +246,11 @@
     dba[:, 128:256] = d_branch[:, 0:128].astype(BF)
     branch[...] = jnp.zeros_like(branch)
     dnorm[...] = jnp.zeros_like(dnorm)
+    pay[...] = jnp.zeros_like(pay)
+    gf[...] = jnp.zeros_like(gf)
+    zt[pl.ds(CHUNK, NZ - CHUNK)] = jnp.zeros((NZ - CHUNK, 8, 128), F32)
+    ztb[pl.ds(CHUNK, NZ - CHUNK)] = jnp.zeros((NZ - CHUNK, 8, 128), BF)
+    v_bout = jnp.sum(d_branch, axis=0, keepdims=True)
     lane8 = lax.broadcasted_iota(jnp.int32, (2 * NZ, 8, 128), 2)
     row8 = lax.broadcasted_iota(jnp.int32, (2 * NZ, 8, 128), 1)
 
@@ -262,11 +274,15 @@
             gather_b[d, k] = launch([
                 copy(band(0, 0, k), band(0, d, k), s_gb.at[i], q_gb.at[i], at_x(d))
             ])
+            if k == 2:
+                i = 3 * d + k
+                gather_c[d, k] = launch([
+                    copy(band(0, 0, k), band(1, d, k), s_gc.at[i], q_gc.at[i], at_xc(NX + d))
+                ])
         pass_on(0, k)
 
     def units(dc, i):
-        two = pl.ds(2 * i, 2)
-        block = wall[dc, two].astype(F32).reshape(2 * NZ, 8, LANES)
+        block = wall[dc, :, pl.ds(HALF * i, HALF)].astype(F32).reshape(2 * NZ, 8, LANES)
         t_a, t_b = block[:, :, 0:128], block[:, :, 128:256]
         tail = jnp.broadcast_to(t_a[:, UNITS : UNITS + 1, :], t_a.shape)
         b_col = jnp.sum(jnp.where(row8 == lane8, tail, 0.0), axis=2, keepdims=True)
@@ -285,7 +301,7 @@
         dnorm[...] += dot(d_pre, win)
 
     def gradients(dc, i):
-        two = pl.ds(2 * i, 2)
+        part_of = pl.ds(HALF * i, HALF)
         hidden, d_pre, normed, db = hid[dc, i], dpb[dc, i], na[...], dba[...]
         dwi = (dot_tn(d_pre, normed) * scale).reshape(2 * NZ, 8, 256)
         dwo = (dot_tn(hidden, db) * scale).reshape(2 * NZ, 8, 256)
@@ -296,28 +312,36 @@
         g_b = jnp.where(lane8 < C - 128, g_b, dwo[:, :, 0:128])
         parts = (g_a, g_b, dwo[:, :, 128:256])
         for j, part in enumerate(parts):
-            part = part.reshape(2, NZ, 8, 128)
+            part = part.reshape(NX, HALF, 8, 128)
             if dc == 0:
-                t1[two, :, :, 128 * j : 128 * j + 128] = part
+                t1[:, part_of, :, 128 * j : 128 * j + 128] = part
             else:
-                swall[two, :, :, 128 * j : 128 * j + 128] = part.astype(BF)
-
-    for k in range(3):
+                swall[:, part_of, :, 128 * j : 128 * j + 128] = part.astype(BF)
+
+    def forward_on(k):
         for d in (1, 3, 2):
             arrive(gather_b[d, k])
-            pass_on(d, k)
-    for i in range(2):
-        units(0, i)
-    for i in range(2):
-        for d in (2 * i, 2 * i + 1):
-            for k in range(3):
-                arrive(gather_c[d, k])
-        units(1, i)
+            if k < 2:
+                pass_on(d, k)
+
+    def arrive_c(k):
+        for d in range(NX):
+            arrive(gather_c[d, k])
+
+    forward_on(0)
+    units(0, 0)
+    forward_on(1)
+    arrive_c(0)
+    units(1, 0)
+    forward_on(2)
+    units(0, 1)
+    arrive_c(1)
+    arrive_c(2)
+    units(1, 1)
 
     cot = cot_ref[...].astype(F32)
     full = jnp.concatenate([branch[:, 128:256], branch[:, 64:128]], axis=1) + bout_ref[...]
     v_gamma = jnp.sum(cot * full, axis=0, keepdims=True)
-    v_bout = jnp.sum(gamma_ref[...] * cot, axis=0, keepdims=True)
 
     dn = dnorm[:, 0:C]
     unit2 = mixed[...]
@@ -343,16 +367,16 @@
         dr, di = df[3 : 3 + SX, top, :], df[3 : 3 + SX, low, :]
         for a in range(W):
             xr, xi = xf[a : a + SX, top, :], xf[a : a + SX, low, :]
-            gf[a, top, :] = jnp.sum(dr * xr + di * xi, axis=0)
-            gf[a, low, :] = jnp.sum(dr * xi - di * xr, axis=0)
+            gf[top, 256 * a : 256 * a + C] = jnp.sum(dr * xr + di * xi, axis=0)
+            gf[low, 256 * a : 256 * a + C] = jnp.sum(dr * xi - di * xr, axis=0)
         return carry
 
     lax.fori_loop(0, NF // 8, grad_step, 0)
-    lag = (lm_ref[0], lm_ref[1])
-    pay[...] = jnp.zeros_like(pay)
+    lag = lm_ref[...]
     vectors = [v_bdw, v_gain, v_bias, v_bout, v_gamma]
+    all_taps = dot3(lag, gf[...]) * scale
     for a in range(W):
-        taps = dot3(lag, gf[a]) * scale
+        taps = all_taps[:, 256 * a : 256 * a + C]
         for b in range(W):
             group = a * W + b
             block = taps[8 * b : 8 * b + 8, :]
@@ -364,8 +388,6 @@
         pay[q, t, W : W + 1, :] = v[:, 0:128] * scale
         pay[r, u, W : W + 1, at : at + C - 128] = v[:, 128:C] * scale
     payb[...] = pay[...].astype(BF)
-    zt[pl.ds(CHUNK, NZ - CHUNK)] = jnp.zeros((NZ - CHUNK, 8, 128), F32)
-    ztb[pl.ds(CHUNK, NZ - CHUNK)] = jnp.zeros((NZ - CHUNK, 8, 128), BF)
 
     def chunk_of(k):
         px = lax.rem(x + k % NX, NX)
@@ -381,8 +403,14 @@
     scatter_c = []
     for i in range(2):
         gradients(1, i)
-        two = pl.ds(2 * i, 2)
-        scatter_c += launch([copy(swall.at[two], r1.at[two], s_rc.at[i], q_rc.at[i], partner)])
+        part_of = pl.ds(HALF * i, HALF)
+        scatter_c += launch([
+            copy(
+                swall.at[d, part_of], r1.at[d, part_of], s_rc.at[NX * i + d], q_rc.at[NX * i + d],
+                partner,
+            )
+            for d in range(NX)
+        ])
     arrive(halo2)
     for p in range(3):
         df[p] = transform(halo_d[0, 64 * p : 64 * p + 64, :]) * has_left
@@ -398,6 +426,7 @@
         return carry
 
     lax.fori_loop(0, NX, add_core, 0)
+    flush()
     scatter_b = launch([
         copy(t1b.at[d], r2.at[d - 1], s_rb.at[d - 1], q_rb.at[d - 1], at_x(-d)) for d in range(1, NX)
     ])
@@ -437,6 +466,7 @@
         t2v = t2v + r2[d].astype(F32)
     t2[...] = t2v
     t2b[...] = t2v.astype(BF)
+    flush()
     scatter_a = launch([
         copy(t2b.at[i], r3.at[i - 1], s_ra.at[i - 1], q_ra.at[i - 1], at_z(-ORDER[i]))
         for i in range(NZ - 1, 0, -1)
@@ -484,8 +514,7 @@
             v_ref[:, 0:128] = first[W : W + 1]
             v_ref[:, 128:C] = second[W : W + 1]
 
-    for c in pending:
-        c.wait_send()
+    flush()
 
 
 def spot(group):
@@ -515,7 +544,7 @@
     vm = pl.BlockSpec(memory_space=pltpu.VMEM)
     hbm = pl.BlockSpec(memory_space=pltpu.HBM)
     dma = pltpu.SemaphoreType.DMA
-    counts = [2, NZ - 1, 9, 12, 2, 2, NX - 1, NZ - 1, 2 * NX - 1, NZ - 1, NZ - 1, 2 * NX - 1]
+    counts = [2, NZ - 1, 9, 12, 2, 2 * NX, NX - 1, NZ - 1, 2 * NX - 1, NZ - 1, NZ - 1, 2 * NX - 1]
     sems = [dma((n,)) for n in counts for _ in range(2)]
     scratch = [pltpu.VMEM(o.shape, o.dtype) for o in operands] + [
         dma((len(operands),)),
@@ -536,7 +565,7 @@
         pltpu.VMEM((SX + 6, 2 * NF, C), F32),
         pltpu.VMEM((SX + 6, 2 * NF, C), F32),
         pltpu.VMEM((SX, 2 * NF, C), F32),
-        pltpu.VMEM((W, 2 * NF, C), F32),
+        pltpu.VMEM((2 * NF, 256 * W), F32),
         pltpu.VMEM((CELLS, C), F32),
         pltpu.VMEM((CELLS, 256), BF),
         pltpu.VMEM((CELLS, 256), BF),

time: 61.5 us -> 61 us (level)
  no operation moved by 1% of the time
where the time goes in v4:
time: 61 us; the launch traced here: 60.9 us
  Pallas kernels  60.2 us (99%)
  between operations  0.66 us (1%)
    pallas_call x1, Pallas kernels, on_device(): pl.pallas_call(kernel_body, out_shape=shapes, in_specs=[hbm] * len(operan...  59.2 us

profile of v4, /device:TPU:1, one launch (start us, length us, event | category | flops | bytes accessed | tf_op | source)
XLA Modules:
  0.0 60.9 jit_solution(4651775131495269153)
XLA Ops:
  0.6 59.2 %shard_map.230 = (bf16[256,192]{1,0:T(8,128)(2,1)S(1)}, bf16[256,192]{1,0:T(8,128)(2,1)S(1)}, f32[7,7,7,192]{3,2,1,0:T(8,128)S(1)}, f32[1,192]{1,0:T(1,128)S(1)}...) custom-call(bf16[256,192]{1,0:T(8,128)(2,1)} %bitcast.16, ...), custom_call_target="tpu_custom_call" | custom-call | tf_op jit(solution)/shard_map/pallas_call | solution.py:598
  59.9 1.0 %shard_map.231 = (bf16[256,192]{1,0:T(8,128)(2,1)}, bf16[256,192]{1,0:T(8,128)(2,1)}, f32[7,7,7,192]{3,2,1,0:T(8,128)}, f32[1,192]{1,0:T(1,128)}, f32[1,192]{1,0...) custom-call(bf16[256,192]{1,0:T(8,128)(2,1)S(1)} %get-tuple-element., ...), custom_call_target="tpu_custom_call" | custom-call | tf_op jit(solution)/shard_map/pallas_call | solution.py:608

commit v5 on v4

--- a/solution.py
+++ b/solution.py
@@ -460,6 +460,16 @@
 
     lax.fori_loop(0, NF // 8, back_step, 0)
 
+    arrive(sum_z)
+    tile = zt[z]
+    for i in range(NZ - 1):
+        tile = tile + rz[i].astype(F32)
+    agz[z] = tile.astype(BF)
+    gather_z = launch([
+        copy(agz.at[z], agz.at[z], s_az.at[i - 1], q_az.at[i - 1], at_z(ORDER[i]))
+        for i in range(NZ - 1, 0, -1)
+    ])
+
     arrive(scatter_b)
     t2v = t1[0]
     for d in range(NX - 1):
@@ -469,16 +479,6 @@
     flush()
     scatter_a = launch([
         copy(t2b.at[i], r3.at[i - 1], s_ra.at[i - 1], q_ra.at[i - 1], at_z(-ORDER[i]))
-        for i in range(NZ - 1, 0, -1)
-    ])
-
-    arrive(sum_z)
-    tile = zt[z]
-    for i in range(NZ - 1):
-        tile = tile + rz[i].astype(F32)
-    agz[z] = tile.astype(BF)
-    gather_z = launch([
-        copy(agz.at[z], agz.at[z], s_az.at[i - 1], q_az.at[i - 1], at_z(ORDER[i]))
         for i in range(NZ - 1, 0, -1)
     ])
 

time: 61 us -> 60.6 us (level)
  no operation moved by 1% of the time
where the time goes in v5:
time: 60.6 us; the launch traced here: 60.4 us
  Pallas kernels  59.8 us (99%)
  between operations  0.66 us (1%)
    pallas_call x1, Pallas kernels, on_device(): pl.pallas_call(kernel_body, out_shape=shapes, in_specs=[hbm] * len(operan...  58.8 us

profile of v5, /device:TPU:1, one launch (start us, length us, event | category | flops | bytes accessed | tf_op | source)
XLA Modules:
  0.0 60.4 jit_solution(1733180753180603605)
XLA Ops:
  0.6 58.8 %shard_map.230 = (bf16[256,192]{1,0:T(8,128)(2,1)S(1)}, bf16[256,192]{1,0:T(8,128)(2,1)S(1)}, f32[7,7,7,192]{3,2,1,0:T(8,128)S(1)}, f32[1,192]{1,0:T(1,128)S(1)}...) custom-call(bf16[256,192]{1,0:T(8,128)(2,1)} %bitcast.16, ...), custom_call_target="tpu_custom_call" | custom-call | tf_op jit(solution)/shard_map/pallas_call | solution.py:598
  59.5 1.0 %shard_map.231 = (bf16[256,192]{1,0:T(8,128)(2,1)}, bf16[256,192]{1,0:T(8,128)(2,1)}, f32[7,7,7,192]{3,2,1,0:T(8,128)}, f32[1,192]{1,0:T(1,128)}, f32[1,192]{1,0...) custom-call(bf16[256,192]{1,0:T(8,128)(2,1)S(1)} %get-tuple-element., ...), custom_call_target="tpu_custom_call" | custom-call | tf_op jit(solution)/shard_map/pallas_call | solution.py:608
